TPU v7x, 32 devices: a whole 2x2x4 slice. The times are simulated.
32 devices in a mesh: dp: 8 (over z, x), fsdp: 4 (over y, core).
Axes of the slice: x: 2, y: 2, z: 4, core: 2. Of those that a mesh axis runs over, the one named last changes fastest.
Arguments:
- inputs: bfloat16 [32, 160, 960], P(('dp', 'fsdp')), may hold values from -6 to 6
- cotangent: bfloat16 [32, 160, 960], P(('dp', 'fsdp')), may hold values from -6 to 6
- w_query: bfloat16 [960, 960], P('fsdp'), may hold values from -0.19364917 to 0.19364917
- key_weight: bfloat16 [960, 320], P('fsdp'), may hold values from -6.5 to 6.5
- value_weight: bfloat16 [960, 320], P('fsdp'), may hold values from -0.1875 to 0.1875
- w_output: bfloat16 [960, 960], P('fsdp'), may hold values from -1 to 1
- w_gate: bfloat16 [960, 2560], P('fsdp'), may hold values from -0.1875 to 0.1875
- w_up: bfloat16 [960, 2560], P('fsdp'), may hold values from -0.1875 to 0.1875
- w_down: bfloat16 [2560, 960], P('fsdp'), may hold values from -0.125 to 0.125
- attn_gain: bfloat16 [960], P('fsdp'), may hold values from 0.5 to 1.5
- mlp_gain: bfloat16 [960], P('fsdp'), may hold values from 0.5 to 1.5
Outputs:
- outputs: bfloat16 [32, 160, 960], P(('dp', 'fsdp'))
- grad_inputs: float32 [32, 160, 960], P(('dp', 'fsdp'))
- grad_w_query: float32 [960, 960], P('fsdp')
- grad_w_key: float32 [960, 320], P('fsdp')
- grad_w_value: float32 [960, 320], P('fsdp')
- grad_w_output: float32 [960, 960], P('fsdp')
- grad_w_gate: float32 [960, 2560], P('fsdp')
- grad_w_up: float32 [960, 2560], P('fsdp')
- grad_w_down: float32 [2560, 960], P('fsdp')
- grad_attn_gain: float32 [960], P('fsdp')
- grad_mlp_gain: float32 [960], P('fsdp')
All inputs are finite; a program needn't handle non-finite values.
Results may differ from a plain program's by a relative error of at most 0.019.
The roundings to bfloat16 on the way count: a program that leaves them out, or rounds other values in their place, can miss the bound.
Values may be sent and summed in bfloat16 or wider, within the bound.
A program may use at most 128 MiB of HBM per device.

v0:
```python
import jax
import jax.numpy as jnp
from jax import lax
from jax.sharding import PartitionSpec as P

QUERY_HEADS = 15
KEY_VALUE_HEADS = 5
HEAD_DIMENSION = 64


EPS = 1e-05
ROPE_BASE = 10000.0


def matrix_product(left_matrix, right_matrix):
    return jnp.dot(left_matrix, right_matrix, preferred_element_type=jnp.float32)


def matmul_tn(left_matrix, right_matrix):
    return lax.dot_general(
        left_matrix, right_matrix, (((0,), (0,)), ((), ())), preferred_element_type=jnp.float32
    )


def matmul_nt(left_matrix, right_matrix):
    return lax.dot_general(
        left_matrix, right_matrix, (((1,), (1,)), ((), ())), preferred_element_type=jnp.float32
    )


def rope_tables(sequence_length, head_size):
    half_size = head_size // 2
    frequency = ROPE_BASE ** (-(jnp.arange(half_size, dtype=jnp.float32) * (2.0 / head_size)))
    angles = jnp.arange(sequence_length, dtype=jnp.float32)[:, None] * frequency[None, :]
    return (jnp.cos(angles), jnp.sin(angles))


def apply_rotary(tensor, cosine_table, sine_lookup, direction):
    half_size = tensor.shape[-1] // 2
    first_half = tensor[..., :half_size]
    second_half = tensor[..., half_size:]
    cos_wide = cosine_table[None, :, None, :]
    sin_wide = sine_lookup[None, :, None, :]
    return jnp.concatenate(
        [
            first_half * cos_wide - direction * second_half * sin_wide,
            second_half * cos_wide + direction * first_half * sin_wide,
        ],
        axis=-1,
    )


def norm_forward(values_in, gain_vec):
    inv_rms = lax.rsqrt(jnp.mean(values_in * values_in, axis=-1, keepdims=True) + EPS)
    unit_rows = values_in * inv_rms
    normed = (unit_rows * gain_vec.astype(jnp.float32)).astype(jnp.bfloat16)
    return (unit_rows, inv_rms, normed)


def norm_backward(grad_out, unit_rows, inv_rms, gain_vec):
    grad_gain = jnp.sum(grad_out * unit_rows, axis=(0, 1))
    grad_unit = grad_out * gain_vec.astype(jnp.float32)
    grad_in = inv_rms * (
        grad_unit - unit_rows * jnp.mean(grad_unit * unit_rows, axis=-1, keepdims=True)
    )
    return (grad_in, grad_gain)


def scores_of(query_rot, key_rot):
    local_sequences, sequence_length, heads_q, head_size = query_rot.shape
    heads_kv = key_rot.shape[2]
    grouped = query_rot.reshape(
        local_sequences, sequence_length, heads_kv, heads_q // heads_kv, head_size
    )
    scores = jnp.einsum(
        "sqhgd,skhd->shgqk", grouped, key_rot, preferred_element_type=jnp.float32
    ) * head_size ** (-0.5)
    positions = jnp.arange(sequence_length)
    allowed = positions[:, None] >= positions[None, :]
    return (grouped, jnp.where(allowed, scores, -1e30))


def attend(query_rot, key_rot, value_low_precision):
    grouped, scores = scores_of(query_rot, key_rot)
    peak_row = jnp.max(scores, axis=-1, keepdims=True)
    logsum = peak_row + jnp.log(jnp.sum(jnp.exp(scores - peak_row), axis=-1, keepdims=True))
    probs_bf = jnp.exp(scores - logsum).astype(jnp.bfloat16)
    attn_mixed = jnp.einsum(
        "shgqk,skhd->sqhgd", probs_bf, value_low_precision, preferred_element_type=jnp.float32
    )
    local_sequences, sequence_length = (query_rot.shape[0], query_rot.shape[1])
    return (attn_mixed.reshape(local_sequences, sequence_length, -1).astype(jnp.bfloat16), logsum)


def attend_back(query_rot, key_rot, value_low_precision, logsum, grad_mixed):
    grouped, scores = scores_of(query_rot, key_rot)
    probs = jnp.exp(scores - logsum)
    probs_bf = probs.astype(jnp.bfloat16)
    grad_grouped = grad_mixed.reshape(grouped.shape)
    value_gradient = jnp.einsum(
        "shgqk,sqhgd->skhd", probs_bf, grad_grouped, preferred_element_type=jnp.float32
    )
    grad_probs = jnp.einsum(
        "sqhgd,skhd->shgqk", grad_grouped, value_low_precision, preferred_element_type=jnp.float32
    )
    row_dot = jnp.sum(probs * grad_probs, axis=-1, keepdims=True)
    grad_scores = (probs * (grad_probs - row_dot) * query_rot.shape[-1] ** (-0.5)).astype(
        jnp.bfloat16
    )
    grad_query = jnp.einsum(
        "shgqk,skhd->sqhgd", grad_scores, key_rot, preferred_element_type=jnp.float32
    )
    key_gradient = jnp.einsum(
        "shgqk,sqhgd->skhd", grad_scores, grouped, preferred_element_type=jnp.float32
    )
    return (grad_query.reshape(query_rot.shape), key_gradient, value_gradient)


def forward_pass(inputs, weights):
    w_query, key_weight, value_weight, w_output, w_gate, w_up, w_down, attn_gain, mlp_gain = weights
    local_sequences, sequence_length, width = inputs.shape
    cosine_table, sine_lookup = rope_tables(sequence_length, HEAD_DIMENSION)
    resid_in = inputs.astype(jnp.float32)
    unit_one, inv_one, normed_one = norm_forward(resid_in, attn_gain)
    flattened_first = normed_one.reshape(-1, width)
    query_proj = matrix_product(flattened_first, w_query).reshape(
        local_sequences, sequence_length, QUERY_HEADS, HEAD_DIMENSION
    )
    projected_key = matrix_product(flattened_first, key_weight).reshape(
        local_sequences, sequence_length, KEY_VALUE_HEADS, HEAD_DIMENSION
    )
    value_low_precision = (
        matrix_product(flattened_first, value_weight)
        .astype(jnp.bfloat16)
        .reshape(local_sequences, sequence_length, KEY_VALUE_HEADS, HEAD_DIMENSION)
    )
    query_rot = apply_rotary(query_proj, cosine_table, sine_lookup, 1.0).astype(jnp.bfloat16)
    key_rot = apply_rotary(projected_key, cosine_table, sine_lookup, 1.0).astype(jnp.bfloat16)
    attn_mixed, logsum = attend(query_rot, key_rot, value_low_precision)
    flat_mixed = attn_mixed.reshape(-1, QUERY_HEADS * HEAD_DIMENSION)
    resid_mid = resid_in + matrix_product(flat_mixed, w_output).reshape(inputs.shape)
    unit_two, inv_two, normed_two = norm_forward(resid_mid, mlp_gain)
    flat_two = normed_two.reshape(-1, width)
    gate_pre = matrix_product(flat_two, w_gate)
    up_proj = matrix_product(flat_two, w_up)
    sigmoid_gate = jax.nn.sigmoid(gate_pre)
    hidden = (gate_pre * sigmoid_gate * up_proj).astype(jnp.bfloat16)
    outputs = (resid_mid + matrix_product(hidden, w_down).reshape(inputs.shape)).astype(
        jnp.bfloat16
    )
    saved = (
        unit_one,
        inv_one,
        flattened_first,
        query_rot,
        key_rot,
        value_low_precision,
        flat_mixed,
        logsum,
        unit_two,
        inv_two,
        flat_two,
        gate_pre,
        up_proj,
        sigmoid_gate,
        hidden,
    )
    return (outputs, saved)


def backward_pass(cotangent, weights, saved):
    w_query, key_weight, value_weight, w_output, w_gate, w_up, w_down, attn_gain, mlp_gain = weights
    (
        unit_one,
        inv_one,
        flattened_first,
        query_rot,
        key_rot,
        value_low_precision,
        flat_mixed,
        logsum,
        unit_two,
        inv_two,
        flat_two,
        gate_pre,
        up_proj,
        sigmoid_gate,
        hidden,
    ) = saved
    local_sequences, sequence_length, width = cotangent.shape
    cosine_table, sine_lookup = rope_tables(sequence_length, HEAD_DIMENSION)
    cot_flat = cotangent.reshape(-1, width)
    sum_down = matmul_tn(hidden, cot_flat)
    grad_hidden = matmul_nt(cot_flat, w_down)
    grad_gate_bf = (
        grad_hidden * up_proj * sigmoid_gate * (1.0 + gate_pre * (1.0 - sigmoid_gate))
    ).astype(jnp.bfloat16)
    grad_up_bf = (grad_hidden * gate_pre * sigmoid_gate).astype(jnp.bfloat16)
    sum_gate = matmul_tn(flat_two, grad_gate_bf)
    sum_up = matmul_tn(flat_two, grad_up_bf)
    grad_normed_two = matmul_nt(grad_gate_bf, w_gate) + matmul_nt(grad_up_bf, w_up)
    grad_norm_two, sum_mlp_gain = norm_backward(
        grad_normed_two.reshape(cotangent.shape), unit_two, inv_two, mlp_gain
    )
    grad_resid_mid = cotangent.astype(jnp.float32) + grad_norm_two
    grad_mid_bf = grad_resid_mid.astype(jnp.bfloat16).reshape(-1, width)
    sum_output = matmul_tn(flat_mixed, grad_mid_bf)
    grad_mixed_bf = (
        matmul_nt(grad_mid_bf, w_output)
        .astype(jnp.bfloat16)
        .reshape(local_sequences, sequence_length, QUERY_HEADS, HEAD_DIMENSION)
    )
    grad_query, key_gradient, value_gradient = attend_back(
        query_rot, key_rot, value_low_precision, logsum, grad_mixed_bf
    )
    grad_query_bf = (
        apply_rotary(grad_query, cosine_table, sine_lookup, -1.0)
        .astype(jnp.bfloat16)
        .reshape(-1, QUERY_HEADS * HEAD_DIMENSION)
    )
    key_gradient_low = (
        apply_rotary(key_gradient, cosine_table, sine_lookup, -1.0)
        .astype(jnp.bfloat16)
        .reshape(-1, KEY_VALUE_HEADS * HEAD_DIMENSION)
    )
    value_gradient_low = value_gradient.astype(jnp.bfloat16).reshape(
        -1, KEY_VALUE_HEADS * HEAD_DIMENSION
    )
    sum_query = matmul_tn(flattened_first, grad_query_bf)
    sum_key = matmul_tn(flattened_first, key_gradient_low)
    sum_value = matmul_tn(flattened_first, value_gradient_low)
    grad_normed_one = (
        matmul_nt(grad_query_bf, w_query)
        + matmul_nt(key_gradient_low, key_weight)
        + matmul_nt(value_gradient_low, value_weight)
    )
    grad_norm_one, sum_attn_gain = norm_backward(
        grad_normed_one.reshape(cotangent.shape), unit_one, inv_one, attn_gain
    )
    grad_inputs = grad_resid_mid + grad_norm_one
    return (
        grad_inputs,
        (
            sum_query,
            sum_key,
            sum_value,
            sum_output,
            sum_gate,
            sum_up,
            sum_down,
            sum_attn_gain,
            sum_mlp_gain,
        ),
    )


def per_device(
    inputs,
    cotangent,
    w_query,
    key_weight,
    value_weight,
    w_output,
    w_gate,
    w_up,
    w_down,
    attn_gain,
    mlp_gain,
):
    gathered = (
        lax.all_gather(w_query, "fsdp", axis=0, tiled=True),
        lax.all_gather(key_weight, "fsdp", axis=0, tiled=True),
        lax.all_gather(value_weight, "fsdp", axis=0, tiled=True),
        lax.all_gather(w_output, "fsdp", axis=0, tiled=True),
        lax.all_gather(w_gate, "fsdp", axis=0, tiled=True),
        lax.all_gather(w_up, "fsdp", axis=0, tiled=True),
        lax.all_gather(w_down, "fsdp", axis=0, tiled=True),
        lax.all_gather(attn_gain, "fsdp", axis=0, tiled=True),
        lax.all_gather(mlp_gain, "fsdp", axis=0, tiled=True),
    )
    outputs, saved = forward_pass(inputs, gathered)
    grad_inputs, grads = backward_pass(cotangent, gathered, saved)
    n_copies = lax.axis_size("dp")
    n_group = lax.axis_size("fsdp")
    scale = float(n_copies * n_group * inputs.shape[0] * inputs.shape[1]) ** (-0.5)
    fsdp_sums = (
        lax.psum_scatter(
            grads[0].astype(jnp.bfloat16), "fsdp", scatter_dimension=0, tiled=True
        ).astype(jnp.float32),
        lax.psum_scatter(
            grads[1].astype(jnp.bfloat16), "fsdp", scatter_dimension=0, tiled=True
        ).astype(jnp.float32),
        lax.psum_scatter(
            grads[2].astype(jnp.bfloat16), "fsdp", scatter_dimension=0, tiled=True
        ).astype(jnp.float32),
        lax.psum_scatter(
            grads[3].astype(jnp.bfloat16), "fsdp", scatter_dimension=0, tiled=True
        ).astype(jnp.float32),
        lax.psum_scatter(
            grads[4].astype(jnp.bfloat16), "fsdp", scatter_dimension=0, tiled=True
        ).astype(jnp.float32),
        lax.psum_scatter(
            grads[5].astype(jnp.bfloat16), "fsdp", scatter_dimension=0, tiled=True
        ).astype(jnp.float32),
        lax.psum_scatter(
            grads[6].astype(jnp.bfloat16), "fsdp", scatter_dimension=0, tiled=True
        ).astype(jnp.float32),
        lax.psum_scatter(
            grads[7].astype(jnp.bfloat16), "fsdp", scatter_dimension=0, tiled=True
        ).astype(jnp.float32),
        lax.psum_scatter(
            grads[8].astype(jnp.bfloat16), "fsdp", scatter_dimension=0, tiled=True
        ).astype(jnp.float32),
    )
    flat_rows = tuple((fsdp_sums[position].reshape(-1) for position in range(7)))
    pieces = (
        lax.psum_scatter(
            flat_rows[0].astype(jnp.bfloat16), "dp", scatter_dimension=0, tiled=True
        ).astype(jnp.float32),
        lax.psum_scatter(
            flat_rows[1].astype(jnp.bfloat16), "dp", scatter_dimension=0, tiled=True
        ).astype(jnp.float32),
        lax.psum_scatter(
            flat_rows[2].astype(jnp.bfloat16), "dp", scatter_dimension=0, tiled=True
        ).astype(jnp.float32),
        lax.psum_scatter(
            flat_rows[3].astype(jnp.bfloat16), "dp", scatter_dimension=0, tiled=True
        ).astype(jnp.float32),
        lax.psum_scatter(
            flat_rows[4].astype(jnp.bfloat16), "dp", scatter_dimension=0, tiled=True
        ).astype(jnp.float32),
        lax.psum_scatter(
            flat_rows[5].astype(jnp.bfloat16), "dp", scatter_dimension=0, tiled=True
        ).astype(jnp.float32),
        lax.psum_scatter(
            flat_rows[6].astype(jnp.bfloat16), "dp", scatter_dimension=0, tiled=True
        ).astype(jnp.float32),
    )
    spread_back = (
        lax.all_gather(pieces[0].astype(jnp.bfloat16), "dp", axis=0, tiled=True).astype(
            jnp.float32
        ),
        lax.all_gather(pieces[1].astype(jnp.bfloat16), "dp", axis=0, tiled=True).astype(
            jnp.float32
        ),
        lax.all_gather(pieces[2].astype(jnp.bfloat16), "dp", axis=0, tiled=True).astype(
            jnp.float32
        ),
        lax.all_gather(pieces[3].astype(jnp.bfloat16), "dp", axis=0, tiled=True).astype(
            jnp.float32
        ),
        lax.all_gather(pieces[4].astype(jnp.bfloat16), "dp", axis=0, tiled=True).astype(
            jnp.float32
        ),
        lax.all_gather(pieces[5].astype(jnp.bfloat16), "dp", axis=0, tiled=True).astype(
            jnp.float32
        ),
        lax.all_gather(pieces[6].astype(jnp.bfloat16), "dp", axis=0, tiled=True).astype(
            jnp.float32
        ),
    )
    matrices = tuple(
        (spread_back[position].reshape(fsdp_sums[position].shape) for position in range(7))
    )
    gain_totals = lax.psum((fsdp_sums[7], fsdp_sums[8]), "dp")
    shards = matrices + (gain_totals[0], gain_totals[1])
    return (
        outputs,
        grad_inputs,
        shards[0] * scale,
        shards[1] * scale,
        shards[2] * scale,
        shards[3] * scale,
        shards[4] * scale,
        shards[5] * scale,
        shards[6] * scale,
        shards[7] * scale,
        shards[8] * scale,
    )


def solution(mesh):
    return jax.shard_map(
        per_device,
        mesh=mesh,
        in_specs=(
            P(("dp", "fsdp"), None, None),
            P(("dp", "fsdp"), None, None),
            P("fsdp", None),
            P("fsdp", None),
            P("fsdp", None),
            P("fsdp", None),
            P("fsdp", None),
            P("fsdp", None),
            P("fsdp", None),
            P("fsdp"),
            P("fsdp"),
        ),
        out_specs=(
            P(("dp", "fsdp"), None, None),
            P(("dp", "fsdp"), None, None),
            P("fsdp", None),
            P("fsdp", None),
            P("fsdp", None),
            P("fsdp", None),
            P("fsdp", None),
            P("fsdp", None),
            P("fsdp", None),
            P("fsdp"),
            P("fsdp"),
        ),
        check_vma=False,
    )
```

profile of v0, /device:TPU:0, one launch (start us, length us, event | category | flops | bytes accessed | tf_op | source)
XLA Modules:
  0.0 897.5 jit_solution(12481011603911108977)
XLA Ops:
  12.4 8.4 all-reduce.14
  20.8 11.5 %all-gather.1 = bf16[4,240,320]{1,2,0:T(8,128)(2,1)S(1)} all-gather(bf16[1,240,320]{1,2,0:T(8,128)(2,1)S(1)} %bitcast.208), channel_id=1, replica_groups=mesh['dp'=8,'fsdp'=4] {'fsdp'}, dimensions={0}, use_global_device_ids=true | all-gather | bytes 768000 | tf_op jit(solution)/shard_map/all_gather | solution.py:272
  33.4 8.0 all-gather
  47.0 4.0 copy.49
  51.0 2.4 convolution_bitcast_fusion
  56.0 5.1 all-gather.17.cloned.1.call-done
  61.1 2.4 multiply_reduce_fusion.2
  64.3 36.9 %all-gather.19.cloned.1.call-done = bf16[960,2560]{1,0:T(8,128)(2,1)} async-done(((bf16[240,2560]{1,0:T(8,128)(2,1)}), bf16[960,2560]{1,0:T(8,128)(2,1)}) %all-gather.19.cloned.1.call-update) | async-done | bytes 4915216 | tf_op jit(solution)/shard_map/all_gather | solution.py:275
  101.3 4.7 fusion.58
  106.0 35.3 %all-gather.21.cloned.1.call-done = bf16[960,2560]{1,0:T(8,128)(2,1)} async-done(((bf16[240,2560]{1,0:T(8,128)(2,1)}), bf16[960,2560]{1,0:T(8,128)(2,1)}) %all-gather.21.cloned.1.call-update) | async-done | bytes 4915216 | tf_op jit(solution)/shard_map/all_gather | solution.py:276
  141.3 4.7 fusion.59
  145.9 35.3 %all-gather.23.cloned.1.call-done = bf16[2560,960]{0,1:T(8,128)(2,1)} async-done(((bf16[640,960]{0,1:T(8,128)(2,1)}), bf16[2560,960]{0,1:T(8,128)(2,1)}) %all-gather.23.cloned.1.call-update) | async-done | bytes 4915216 | tf_op jit(solution)/shard_map/all_gather | solution.py:277
  181.2 5.7 multiply_convert_fusion
  187.0 4.7 fusion.60
  191.7 2.2 fusion.22
  195.7 1.5 convolution_convert_fusion.8
  197.2 2.0 copy.51
  199.2 1.6 fusion.10
  200.9 2.0 fusion
  204.2 2.2 copy.71
  206.5 2.3 fusion.8
  212.5 1.9 convolution_convert_fusion.3
  216.1 2.1 convolution_convert_fusion.4
  218.3 3.7 convolution_convert_fusion.2
  223.2 3.6 convolution_convert_fusion.1
  228.1 3.8 convolution_convert_fusion
  231.8 7.9 copy.73
  239.8 1.8 convert_element_type.266
  241.7 13.3 %reduce-scatter.22.cloned.1.call-done = bf16[240,320]{1,0:T(8,128)(2,1)} async-done(((bf16[960,320]{1,0:T(8,128)(2,1)}), bf16[240,320]{1,0:T(8,128)(2,1)}) %reduce-scatter.22.cloned.1.call-update) | async-done | bytes 153616 | tf_op jit(solution)/shard_map/reduce_scatter | solution.py:290
  255.0 1.8 convert_element_type.263
  256.9 31.7 %reduce-scatter.16.cloned.1.call-done = bf16[240,960]{1,0:T(8,128)(2,1)} async-done(((bf16[960,960]{1,0:T(8,128)(2,1)}), bf16[240,960]{1,0:T(8,128)(2,1)}) %reduce-scatter.16.cloned.1.call-update) | async-done | bytes 460816 | tf_op jit(solution)/shard_map/reduce_scatter | solution.py:296
  288.6 2.4 convert_element_type.269
  291.0 31.2 %reduce-scatter.14.cloned.1.call-done = bf16[240,960]{1,0:T(8,128)(2,1)} async-done(((bf16[960,960]{1,0:T(8,128)(2,1)}), bf16[240,960]{1,0:T(8,128)(2,1)}) %reduce-scatter.14.cloned.1.call-update) | async-done | bytes 460816 | tf_op jit(solution)/shard_map/reduce_scatter | solution.py:287
  322.2 2.4 convert_element_type.260
  324.5 49.3 %reduce-scatter.18.cloned.1.call-done = bf16[240,2560]{1,0:T(8,128)(2,1)} async-done(((bf16[960,2560]{1,0:T(8,128)(2,1)}), bf16[240,2560]{1,0:T(8,128)(2,1)}) %reduce-scatter.18.cloned.1.call-update) | async-done | bytes 1228816 | tf_op jit(solution)/shard_map/reduce_scatter | solution.py:299
  373.8 3.7 convert_element_type.272
  377.5 48.1 %reduce-scatter.20.cloned.1.call-done = bf16[240,2560]{1,0:T(8,128)(2,1)} async-done(((bf16[960,2560]{1,0:T(8,128)(2,1)}), bf16[240,2560]{1,0:T(8,128)(2,1)}) %reduce-scatter.20.cloned.1.call-update) | async-done | bytes 1228816 | tf_op jit(solution)/shard_map/reduce_scatter | solution.py:302
  425.7 3.7 convert_element_type.275
  429.4 50.0 %reduce-scatter.26.cloned.1.call-done = bf16[640,960]{1,0:T(8,128)(2,1)} async-done(((bf16[2560,960]{1,0:T(8,128)(2,1)}), bf16[640,960]{1,0:T(8,128)(2,1)}) %reduce-scatter.26.cloned.1.call-update) | async-done | bytes 1228816 | tf_op jit(solution)/shard_map/reduce_scatter | solution.py:305
  479.4 3.8 convert_element_type.278
  485.1 175.4 %all-reduce.17.cloned.1.call-done = (bf16[230400]{0:T(1024)(128)(2,1)}, bf16[76800]{0:T(1024)(128)(2,1)}, bf16[76800]{0:T(1024)(128)(2,1)}, bf16[230400]{0:T(102...) async-done(((bf16[230400]{0:T(1024)(128)(2,1)}, bf16[76800]{0:T(1024)(128)(2,1)}, bf16[76800]{0:T(1024)(128)(2,1)}, ...) | async-done | bytes 4915216
  660.5 1.6 dynamic-slice.15
  664.6 2.4 fusion.61
  667.9 6.4 all-reduce.13
  674.4 19.9 %all-reduce.11 = (f32[240]{0:T(256)S(1)}, f32[240]{0:T(256)S(1)}) all-reduce(f32[240]{0:T(256)S(1)} %get-tuple-element.75, f32[240]{0:T(256)S(1)} %get-tuple-element.74), channel_id=1, replica_groups=mesh['dp'=8,'fsdp'=4] {'dp'}, use_global_device_ids=true, to_apply=%region_23.24 | all-reduce | flops 480 | bytes 3840 | tf_op jit(solution)/shard_map/psum | solution.py:365
  695.5 1.6 dynamic-slice.11
  698.2 4.8 fusion.9
  703.0 1.6 dynamic-slice.13
  705.6 33.7 %all-gather.5 = bf16[8,1,28800]{2,1,0:T(2,128)(2,1)S(1)} all-gather(bf16[1,1,28800]{2,1,0:T(2,128)(2,1)S(1)} %reshape.418), channel_id=1, replica_groups=mesh['dp'=8,'fsdp'=4] {'dp'}, dimensions={0}, use_global_device_ids=true | all-gather | bytes 518400 | tf_op jit(solution)/shard_map/all_gather | solution.py:349
  739.4 2.9 multiply_reduce_fusion
  742.2 1.3 mul.562
  744.6 32.5 %all-gather.2 = bf16[8,1,28800]{2,1,0:T(2,128)(2,1)S(1)} all-gather(bf16[1,1,28800]{2,1,0:T(2,128)(2,1)S(1)} %reshape.412), channel_id=1, replica_groups=mesh['dp'=8,'fsdp'=4] {'dp'}, dimensions={0}, use_global_device_ids=true | all-gather | bytes 518400 | tf_op jit(solution)/shard_map/all_gather | solution.py:340
  777.1 2.9 multiply_reduce_fusion.1
  779.9 1.3 mul.556
  782.1 31.0 %all-gather.3 = bf16[8,1,9600]{2,1,0:T(2,128)(2,1)S(1)} all-gather(bf16[1,1,9600]{2,1,0:T(2,128)(2,1)S(1)} %reshape.414), channel_id=1, replica_groups=mesh['dp'=8,'fsdp'=4] {'dp'}, dimensions={0}, use_global_device_ids=true | all-gather | bytes 172800 | tf_op jit(solution)/shard_map/all_gather | solution.py:343
  816.0 31.0 %all-gather.4 = bf16[8,1,9600]{2,1,0:T(2,128)(2,1)S(1)} all-gather(bf16[1,1,9600]{2,1,0:T(2,128)(2,1)S(1)} %reshape.416), channel_id=1, replica_groups=mesh['dp'=8,'fsdp'=4] {'dp'}, dimensions={0}, use_global_device_ids=true | all-gather | bytes 172800 | tf_op jit(solution)/shard_map/all_gather | solution.py:346
  849.1 1.5 convert_multiply_fusion
  850.6 2.9 convert_multiply_fusion.2
  853.5 1.9 mul.568
  855.4 3.3 copy.60
  858.7 1.6 mul.564
  860.4 27.3 %all-gather.27.cloned.1.call-done = bf16[614400]{0:T(1024)(128)(2,1)} async-done(((bf16[76800]{0:T(1024)(128)(2,1)}), bf16[614400]{0:T(1024)(128)(2,1)}) %all-gather.27.cloned.1.call-update) | async-done | bytes 1228816 | tf_op jit(solution)/shard_map/all_gather | solution.py:355
  887.6 1.5 convert_multiply_fusion.1
  889.1 1.6 mul.566
  (202 shorter events, 38.0 us)
Async XLA Ops:
  7.2 3.5 copy-start.49
  7.2 4.7 copy-start.50
  7.2 5.0 copy-start.51
  7.2 13.6 %copy-start.34 = (bf16[240,320]{0,1:T(8,128)(2,1)S(1)}, bf16[240,320]{0,1:T(8,128)(2,1)}, u32[]{:S(2)}) copy-start(bf16[240,320]{0,1:T(8,128)(2,1)} %param.14) | copy-start | bytes 460804
  7.2 39.8 %all-gather.15.cloned.1.call-start = ((), (), s32[]{:S(2)}) async-start(), calls=%async_computation.7 | async-start | bytes 2457600 | tf_op jit(solution)/shard_map/all_gather | solution.py:271
  8.0 53.2 %all-gather.17.cloned.1.call-start = ((), (), s32[]{:S(2)}) async-start(), calls=%async_computation.8 | async-start | bytes 2457600 | tf_op jit(solution)/shard_map/all_gather | solution.py:274
  8.7 92.6 %all-gather.19.cloned.1.call-start = ((), (), s32[]{:S(2)}) async-start(), calls=%async_computation.9 | async-start | bytes 6144000 | tf_op jit(solution)/shard_map/all_gather | solution.py:275
  9.4 131.8 %all-gather.21.cloned.1.call-start = ((), (), s32[]{:S(2)}) async-start(), calls=%async_computation.10 | async-start | bytes 6144000 | tf_op jit(solution)/shard_map/all_gather | solution.py:276
  10.0 23.3 %copy-start.35 = (bf16[240,320]{0,1:T(8,128)(2,1)S(1)}, bf16[240,320]{0,1:T(8,128)(2,1)}, u32[]{:S(2)}) copy-start(bf16[240,320]{0,1:T(8,128)(2,1)} %param.15) | copy-start | bytes 460804
  10.0 171.2 %all-gather.23.cloned.1.call-start = ((), (), s32[]{:S(2)}) async-start(), calls=%async_computation.11 | async-start | bytes 6144000 | tf_op jit(solution)/shard_map/all_gather | solution.py:277
  10.6 229.2 %reduce-scatter.24.cloned.1.call-start = ((), (), s32[]{:S(2)}) async-start(), calls=%async_computation.20 | async-start | bytes 921600 | tf_op jit(solution)/shard_map/reduce_scatter | solution.py:293
  20.8 30.2 %copy-start.36 = (f32[960]{0:T(1024)}, f32[960]{0:T(1024)S(1)}, u32[]{:S(2)}) copy-start(f32[960]{0:T(1024)S(1)} %convert_element_type.234) | copy-start | bytes 11524
  32.8 9.6 %copy-start.1 = (bf16[1,160,960]{2,1,0:T(8,128)(2,1)S(1)}, bf16[1,160,960]{2,1,0:T(8,128)(2,1)}, u32[]{:S(2)}) copy-start(bf16[1,160,960]{2,1,0:T(8,128)(2,1)} %param.11) | copy-start | bytes 921604
  33.3 11.7 %copy-start.16 = (bf16[960,320]{0,1:T(8,128)(2,1)}, bf16[960,320]{0,1:T(8,128)(2,1)S(1)}, u32[]{:S(2)}) copy-start(bf16[960,320]{0,1:T(8,128)(2,1)S(1)} %reshape.411) | copy-start | bytes 1843204
  42.4 8.6 copy-start.18
  42.6 8.4 copy-start.43
  47.0 6.6 copy-start.30
  51.0 2.6 copy-start.31
  51.0 2.6 copy-start.42
  53.5 1.1 copy-start.26
  53.6 1.1 copy-start.28
  53.6 1.1 copy-start.20
  56.0 7.5 copy-start.41
  187.0 4.7 copy-start.14
  187.0 4.7 copy-start.12
  187.0 4.7 copy-start
  191.7 2.2 copy-start.24
  193.9 1.8 copy-start.8
  199.2 1.7 copy-start.11
  199.2 1.7 copy-start.21
  200.8 2.1 copy-start.22
  200.9 2.0 copy-start.37
  200.9 2.0 copy-start.44
  206.4 48.6 %reduce-scatter.22.cloned.1.call-start = ((), (), s32[]{:S(2)}) async-start(), calls=%async_computation.19 | async-start | bytes 921600 | tf_op jit(solution)/shard_map/reduce_scatter | solution.py:290
  206.5 3.4 copy-start.27
  206.5 3.4 copy-start.29
  206.5 3.9 copy-start.32
  208.9 1.0 copy-start.3
  210.4 2.1 copy-start.6
  210.4 2.0 copy-start.10
  212.2 2.3 copy-start.4
  212.2 76.4 %reduce-scatter.16.cloned.1.call-start = ((), (), s32[]{:S(2)}) async-start(), calls=%async_computation.13 | async-start | bytes 2457600 | tf_op jit(solution)/shard_map/reduce_scatter | solution.py:296
  214.4 1.4 copy-start.33
  214.5 107.7 %reduce-scatter.14.cloned.1.call-start = ((), (), s32[]{:S(2)}) async-start(), calls=%async_computation.12 | async-start | bytes 2457600 | tf_op jit(solution)/shard_map/reduce_scatter | solution.py:287
  214.5 1.6 copy-start.39
  214.5 1.6 copy-start.46
  216.1 2.2 copy-start.2
  216.1 2.2 copy-start.15
  218.2 155.6 %reduce-scatter.18.cloned.1.call-start = ((), (), s32[]{:S(2)}) async-start(), calls=%async_computation.14 | async-start | bytes 6144000 | tf_op jit(solution)/shard_map/reduce_scatter | solution.py:299
  222.0 1.2 copy-start.13
  222.1 203.6 %reduce-scatter.20.cloned.1.call-start = ((), (), s32[]{:S(2)}) async-start(), calls=%async_computation.16 | async-start | bytes 6144000 | tf_op jit(solution)/shard_map/reduce_scatter | solution.py:302
  226.8 1.1 copy-start.9
  226.8 1.2 copy-start.25
  226.9 252.6 %reduce-scatter.26.cloned.1.call-start = ((), (), s32[]{:S(2)}) async-start(), calls=%async_computation.21 | async-start | bytes 6553600 | tf_op jit(solution)/shard_map/reduce_scatter | solution.py:305
  239.8 420.7 %all-reduce.17.cloned.1.call-start = ((), (), s32[]{:S(2)}) async-start(), calls=%async_computation.22 | async-start | bytes 9830400
  483.2 365.9 %all-gather.29.cloned.1.call-start = ((), (), s32[]{:S(2)}) async-start(), calls=%async_computation.18 | async-start | bytes 1382400 | tf_op jit(solution)/shard_map/all_gather | solution.py:358
  662.1 188.5 %all-gather.25.cloned.1.call-start = ((), (), s32[]{:S(2)}) async-start(), calls=%async_computation.15 | async-start | bytes 1382400 | tf_op jit(solution)/shard_map/all_gather | solution.py:352
  664.5 2.5 copy-start.17
  664.5 2.8 copy-start.19
  664.5 2.8 copy-start.23
  664.5 2.8 copy-start.40
  664.5 2.8 copy-start.47
  697.1 190.5 %all-gather.27.cloned.1.call-start = ((), (), s32[]{:S(2)}) async-start(), calls=%async_computation.17 | async-start | bytes 1382400 | tf_op jit(solution)/shard_map/all_gather | solution.py:355
  855.4 3.3 copy-start.7
  (5 other events, 3.8 us)
Sparse Core Ops, SparseCore 0:
  9.6 28.0 all-gather.14
  39.2 21.8 all-gather.16
  62.7 38.5 all-gather.18
  102.7 38.5 all-gather.20
  142.7 38.4 all-gather.22
  206.6 22.9 reduce-scatter.23
  232.1 22.9 reduce-scatter.21
  258.2 30.3 reduce-scatter.15
  291.7 30.3 reduce-scatter.13
  324.6 49.2 reduce-scatter.17
  376.4 49.2 reduce-scatter.19
  428.1 51.3 reduce-scatter.25
  485.2 175.2 all-reduce.16
  663.1 40.3 all-gather.28
  706.2 46.5 all-gather.24
  849.2 38.3 all-gather.26
where the time goes:
time: 903 us; the launch traced here: 897 us
  waiting for transfers between devices  542 us (60%)
  blocking collectives  182 us (20%)
  local copies, waits for them, and re-layouts  68.7 us (8%)
  matrix products  61.5 us (7%)
  other arithmetic  23 us (3%)
  between operations  18.2 us (2%)
    unnamed x17, waiting for transfers between devices  179 us
    reduce_scatter x1, waiting for transfers between devices, per_device(): lax.psum_scatter(grads[6].astype(jnp.bfloat16), 'fsdp', scatter_dimension...  50 us
    reduce_scatter x1, waiting for transfers between devices, per_device(): lax.psum_scatter(grads[4].astype(jnp.bfloat16), 'fsdp', scatter_dimension...  49.3 us
    reduce_scatter x1, waiting for transfers between devices, per_device(): lax.psum_scatter(grads[5].astype(jnp.bfloat16), 'fsdp', scatter_dimension...  48.1 us
    all_gather x1, waiting for transfers between devices, per_device(): lax.all_gather(w_gate, 'fsdp', axis=0, tiled=True)  36.9 us
    all_gather x1, waiting for transfers between devices, per_device(): lax.all_gather(w_up, 'fsdp', axis=0, tiled=True)  35.3 us
    all_gather x1, waiting for transfers between devices, per_device(): lax.all_gather(w_down, 'fsdp', axis=0, tiled=True)  35.3 us
    all_gather x1, blocking collectives, per_device(): lax.all_gather(pieces[3].astype(jnp.bfloat16), 'dp', axis=0, tiled=True)  33.7 us
  transfers between devices with their start and end apart: 16, of which 12 were waited for; matrix products, arithmetic and copies ran while one was open for 13% of the time, Pallas kernels for 0%

commit v1 on v0

--- a/solution.py
+++ b/solution.py
@@ -1,6 +1,10 @@
+import functools
+
 import jax
 import jax.numpy as jnp
 from jax import lax
+from jax.experimental import pallas as pl
+from jax.experimental.pallas import tpu as pltpu
 from jax.sharding import PartitionSpec as P
 
 QUERY_HEADS = 15
@@ -190,7 +194,7 @@
     local_sequences, sequence_length, width = cotangent.shape
     cosine_table, sine_lookup = rope_tables(sequence_length, HEAD_DIMENSION)
     cot_flat = cotangent.reshape(-1, width)
-    sum_down = matmul_tn(hidden, cot_flat)
+    sum_down = matmul_tn(cot_flat, hidden)
     grad_hidden = matmul_nt(cot_flat, w_down)
     grad_gate_bf = (
         grad_hidden * up_proj * sigmoid_gate * (1.0 + gate_pre * (1.0 - sigmoid_gate))
@@ -252,6 +256,292 @@
             sum_mlp_gain,
         ),
     )
+
+
+CHUNK = 512
+
+
+def dp_split(n_copies):
+    outer = 4 if n_copies % 4 == 0 else 1
+    return n_copies // outer, outer
+
+
+def reduce_kernel(n_copies, n_group, n_blocks, per_block, *refs):
+    sources = refs[:n_blocks]
+    out_hbm = refs[n_blocks]
+    own, from_core, from_pair, from_inner, from_outer, final = refs[n_blocks + 1 : n_blocks + 7]
+    (load_sem, store_sem, send_core, recv_core, send_pair, recv_pair, send_in, recv_in,
+     send_out, recv_out, send_ago, recv_ago, send_agi, recv_agi) = refs[n_blocks + 7 :]
+    inner_n, outer_n = dp_split(n_copies)
+    pair_n = n_group // 2
+    steps = n_blocks * per_block
+    copy_id = lax.axis_index("dp")
+    member = lax.axis_index("fsdp")
+    pair, core = member // 2, member % 2
+    outer, inner = copy_id // inner_n, copy_id % inner_n
+    piece = CHUNK // outer_n
+
+    def pair_peer(k):
+        return (pair + k) % pair_n
+
+    def inner_peer(k):
+        return (inner + k) % inner_n
+
+    def outer_peer(k):
+        return (outer + k) % outer_n
+
+    def columns(z):
+        return pl.ds(pl.multiple_of(z * piece, piece), piece)
+
+    core_device = (copy_id, pair * 2 + (1 - core))
+    barrier = pltpu.get_barrier_semaphore()
+    devices = [core_device]
+    devices += [(copy_id, pair_peer(k) * 2 + core) for k in range(1, pair_n)]
+    devices += [(outer * inner_n + inner_peer(k), member) for k in range(1, inner_n)]
+    devices += [(outer_peer(k) * inner_n + inner, member) for k in range(1, outer_n)]
+    for device in devices:
+        pl.semaphore_signal(
+            barrier, inc=1, device_id=device, device_id_type=pl.DeviceIdType.MESH
+        )
+    pl.semaphore_wait(barrier, len(devices))
+
+    def remote(src, dst, send, recv, device):
+        return pltpu.make_async_remote_copy(
+            src_ref=src,
+            dst_ref=dst,
+            send_sem=send,
+            recv_sem=recv,
+            device_id=device,
+            device_id_type=pl.DeviceIdType.MESH,
+        )
+
+    def core_copy(t, source, c):
+        cols = pl.ds(c * CHUNK, CHUNK)
+        return remote(
+            source.at[:, 1 - core, :, :, cols],
+            from_core.at[t],
+            send_core.at[t],
+            recv_core.at[t],
+            core_device,
+        )
+
+    def load_copy(t, source, c):
+        cols = pl.ds(c * CHUNK, CHUNK)
+        return pltpu.make_async_copy(
+            source.at[:, core, :, :, cols], own.at[t], load_sem.at[t]
+        )
+
+    def pair_copy(t, k):
+        return remote(
+            own.at[t, pair_peer(k)],
+            from_pair.at[t, k - 1],
+            send_pair.at[t, k - 1],
+            recv_pair.at[t, k - 1],
+            (copy_id, pair_peer(k) * 2 + core),
+        )
+
+    def inner_copy(t, k):
+        return remote(
+            own.at[t, pair, inner_peer(k)],
+            from_inner.at[t, k - 1],
+            send_in.at[t, k - 1],
+            recv_in.at[t, k - 1],
+            (outer * inner_n + inner_peer(k), member),
+        )
+
+    def outer_copy(t, k):
+        return remote(
+            own.at[t, pair, inner, :, columns(outer_peer(k))],
+            from_outer.at[t, k - 1],
+            send_out.at[t, k - 1],
+            recv_out.at[t, k - 1],
+            (outer_peer(k) * inner_n + inner, member),
+        )
+
+    def spread_outer(t, k):
+        place = final.at[t, inner, :, columns(outer)]
+        return remote(
+            place,
+            place,
+            send_ago.at[t, k - 1],
+            recv_ago.at[t, k - 1],
+            (outer_peer(k) * inner_n + inner, member),
+        )
+
+    def landed_outer(t, k):
+        place = final.at[t, inner, :, columns((outer + outer_n - k) % outer_n)]
+        return remote(
+            place,
+            place,
+            send_ago.at[t, k - 1],
+            recv_ago.at[t, k - 1],
+            (outer_peer(k) * inner_n + inner, member),
+        )
+
+    def spread_inner(t, k):
+        place = final.at[t, inner]
+        return remote(
+            place,
+            place,
+            send_agi.at[t, k - 1],
+            recv_agi.at[t, k - 1],
+            (outer * inner_n + inner_peer(k), member),
+        )
+
+    def landed_inner(t, k):
+        place = final.at[t, (inner + inner_n - k) % inner_n]
+        return remote(
+            place,
+            place,
+            send_agi.at[t, k - 1],
+            recv_agi.at[t, k - 1],
+            (outer * inner_n + inner_peer(k), member),
+        )
+
+    def store_copy(t):
+        return pltpu.make_async_copy(final.at[t], out_hbm.at[t], store_sem.at[t])
+
+    for t in range(steps):
+        core_copy(t, sources[t // per_block], t % per_block).start()
+        load_copy(t, sources[t // per_block], t % per_block).start()
+
+    def stage_core(t):
+        core_copy(t, sources[0], 0).wait_recv()
+        load_copy(t, sources[0], 0).wait()
+
+        def add(i, carry):
+            p, x = i // inner_n, i % inner_n
+            total = own[t, p, x].astype(jnp.float32) + from_core[t, p, x].astype(jnp.float32)
+            own[t, p, x] = total.astype(own.dtype)
+            return carry
+
+        lax.fori_loop(0, pair_n * inner_n, add, 0)
+        for k in range(1, pair_n):
+            pair_copy(t, k).start()
+
+    def stage_pair(t):
+        for k in range(1, pair_n):
+            pair_copy(t, k).wait_recv()
+
+        def add(x, carry):
+            total = own[t, pair, x].astype(jnp.float32)
+            for k in range(1, pair_n):
+                total += from_pair[t, k - 1, x].astype(jnp.float32)
+            own[t, pair, x] = total.astype(own.dtype)
+            return carry
+
+        lax.fori_loop(0, inner_n, add, 0)
+        for k in range(1, inner_n):
+            inner_copy(t, k).start()
+
+    def stage_inner(t):
+        total = own[t, pair, inner].astype(jnp.float32)
+        for k in range(1, inner_n):
+            inner_copy(t, k).wait_recv()
+            total += from_inner[t, k - 1].astype(jnp.float32)
+        own[t, pair, inner] = total.astype(own.dtype)
+        for k in range(1, outer_n):
+            outer_copy(t, k).start()
+
+    def stage_outer(t):
+        total = own[t, pair, inner, :, columns(outer)].astype(jnp.float32)
+        for k in range(1, outer_n):
+            outer_copy(t, k).wait_recv()
+            total += from_outer[t, k - 1].astype(jnp.float32)
+        final[t, inner, :, columns(outer)] = total.astype(final.dtype)
+        for k in range(1, outer_n):
+            spread_outer(t, k).start()
+
+    def stage_spread(t):
+        for k in range(1, outer_n):
+            landed_outer(t, k).wait_recv()
+        for k in range(1, inner_n):
+            spread_inner(t, k).start()
+
+    def stage_store(t):
+        for k in range(1, inner_n):
+            landed_inner(t, k).wait_recv()
+        store_copy(t).start()
+
+    lags = ((stage_core, 0), (stage_pair, 4), (stage_inner, 6), (stage_outer, 8),
+            (stage_spread, 10), (stage_store, 12))
+
+    def step(s, carry):
+        for stage, lag in lags:
+            @pl.when((s >= lag) & (s < steps + lag))
+            def _():
+                stage(s - lag)
+        return carry
+
+    lax.fori_loop(0, steps + 12, step, 0)
+
+    def drain(t, carry):
+        core_copy(t, sources[0], 0).wait_send()
+        for k in range(1, pair_n):
+            pair_copy(t, k).wait_send()
+        for k in range(1, inner_n):
+            inner_copy(t, k).wait_send()
+            spread_inner(t, k).wait_send()
+        for k in range(1, outer_n):
+            outer_copy(t, k).wait_send()
+            spread_outer(t, k).wait_send()
+        store_copy(t).wait()
+        return carry
+
+    lax.fori_loop(0, steps, drain, 0)
+
+
+def reduce_blocks(blocks, n_copies, n_group):
+    n_blocks = len(blocks)
+    total_rows, total_columns = blocks[0].shape
+    inner_n, outer_n = dp_split(n_copies)
+    pair_n = n_group // 2
+    part = total_rows // (n_group * inner_n)
+    per_block = total_columns // CHUNK
+    steps = n_blocks * per_block
+    piece = CHUNK // outer_n
+    bf = jnp.bfloat16
+    dma = pltpu.SemaphoreType.DMA
+
+    def many(n):
+        return dma((steps, max(n - 1, 1)))
+
+    gathered = pl.pallas_call(
+        functools.partial(reduce_kernel, n_copies, n_group, n_blocks, per_block),
+        out_shape=jax.ShapeDtypeStruct((steps, inner_n, part, CHUNK), bf),
+        in_specs=[pl.BlockSpec(memory_space=pl.ANY)] * n_blocks,
+        out_specs=pl.BlockSpec(memory_space=pl.ANY),
+        scratch_shapes=[
+            pltpu.VMEM((steps, pair_n, inner_n, part, CHUNK), bf),
+            pltpu.VMEM((steps, pair_n, inner_n, part, CHUNK), bf),
+            pltpu.VMEM((steps, max(pair_n - 1, 1), inner_n, part, CHUNK), bf),
+            pltpu.VMEM((steps, max(inner_n - 1, 1), part, CHUNK), bf),
+            pltpu.VMEM((steps, max(outer_n - 1, 1), part, piece), bf),
+            pltpu.VMEM((steps, inner_n, part, CHUNK), bf),
+            dma((steps,)),
+            dma((steps,)),
+            dma((steps,)),
+            dma((steps,)),
+            many(pair_n),
+            many(pair_n),
+            many(inner_n),
+            many(inner_n),
+            many(outer_n),
+            many(outer_n),
+            many(outer_n),
+            many(outer_n),
+            many(inner_n),
+            many(inner_n),
+        ],
+        compiler_params=pltpu.CompilerParams(
+            collective_id=0, has_side_effects=True, vmem_limit_bytes=60 * 1024 * 1024
+        ),
+    )(*(b.reshape(pair_n, 2, inner_n, part, total_columns) for b in blocks))
+    gathered = gathered.reshape(n_blocks, per_block, inner_n * part, CHUNK)
+    return [
+        gathered[b].transpose(1, 0, 2).reshape(inner_n * part, total_columns)
+        for b in range(n_blocks)
+    ]
 
 
 def per_device(
@@ -283,99 +573,41 @@
     n_copies = lax.axis_size("dp")
     n_group = lax.axis_size("fsdp")
     scale = float(n_copies * n_group * inputs.shape[0] * inputs.shape[1]) ** (-0.5)
-    fsdp_sums = (
-        lax.psum_scatter(
-            grads[0].astype(jnp.bfloat16), "fsdp", scatter_dimension=0, tiled=True
-        ).astype(jnp.float32),
-        lax.psum_scatter(
-            grads[1].astype(jnp.bfloat16), "fsdp", scatter_dimension=0, tiled=True
-        ).astype(jnp.float32),
-        lax.psum_scatter(
-            grads[2].astype(jnp.bfloat16), "fsdp", scatter_dimension=0, tiled=True
-        ).astype(jnp.float32),
-        lax.psum_scatter(
-            grads[3].astype(jnp.bfloat16), "fsdp", scatter_dimension=0, tiled=True
-        ).astype(jnp.float32),
-        lax.psum_scatter(
-            grads[4].astype(jnp.bfloat16), "fsdp", scatter_dimension=0, tiled=True
-        ).astype(jnp.float32),
-        lax.psum_scatter(
-            grads[5].astype(jnp.bfloat16), "fsdp", scatter_dimension=0, tiled=True
-        ).astype(jnp.float32),
-        lax.psum_scatter(
-            grads[6].astype(jnp.bfloat16), "fsdp", scatter_dimension=0, tiled=True
-        ).astype(jnp.float32),
-        lax.psum_scatter(
-            grads[7].astype(jnp.bfloat16), "fsdp", scatter_dimension=0, tiled=True
-        ).astype(jnp.float32),
-        lax.psum_scatter(
-            grads[8].astype(jnp.bfloat16), "fsdp", scatter_dimension=0, tiled=True
-        ).astype(jnp.float32),
-    )
-    flat_rows = tuple((fsdp_sums[position].reshape(-1) for position in range(7)))
-    pieces = (
-        lax.psum_scatter(
-            flat_rows[0].astype(jnp.bfloat16), "dp", scatter_dimension=0, tiled=True
-        ).astype(jnp.float32),
-        lax.psum_scatter(
-            flat_rows[1].astype(jnp.bfloat16), "dp", scatter_dimension=0, tiled=True
-        ).astype(jnp.float32),
-        lax.psum_scatter(
-            flat_rows[2].astype(jnp.bfloat16), "dp", scatter_dimension=0, tiled=True
-        ).astype(jnp.float32),
-        lax.psum_scatter(
-            flat_rows[3].astype(jnp.bfloat16), "dp", scatter_dimension=0, tiled=True
-        ).astype(jnp.float32),
-        lax.psum_scatter(
-            flat_rows[4].astype(jnp.bfloat16), "dp", scatter_dimension=0, tiled=True
-        ).astype(jnp.float32),
-        lax.psum_scatter(
-            flat_rows[5].astype(jnp.bfloat16), "dp", scatter_dimension=0, tiled=True
-        ).astype(jnp.float32),
-        lax.psum_scatter(
-            flat_rows[6].astype(jnp.bfloat16), "dp", scatter_dimension=0, tiled=True
-        ).astype(jnp.float32),
-    )
-    spread_back = (
-        lax.all_gather(pieces[0].astype(jnp.bfloat16), "dp", axis=0, tiled=True).astype(
-            jnp.float32
-        ),
-        lax.all_gather(pieces[1].astype(jnp.bfloat16), "dp", axis=0, tiled=True).astype(
-            jnp.float32
-        ),
-        lax.all_gather(pieces[2].astype(jnp.bfloat16), "dp", axis=0, tiled=True).astype(
-            jnp.float32
-        ),
-        lax.all_gather(pieces[3].astype(jnp.bfloat16), "dp", axis=0, tiled=True).astype(
-            jnp.float32
-        ),
-        lax.all_gather(pieces[4].astype(jnp.bfloat16), "dp", axis=0, tiled=True).astype(
-            jnp.float32
-        ),
-        lax.all_gather(pieces[5].astype(jnp.bfloat16), "dp", axis=0, tiled=True).astype(
-            jnp.float32
-        ),
-        lax.all_gather(pieces[6].astype(jnp.bfloat16), "dp", axis=0, tiled=True).astype(
-            jnp.float32
-        ),
-    )
-    matrices = tuple(
-        (spread_back[position].reshape(fsdp_sums[position].shape) for position in range(7))
-    )
-    gain_totals = lax.psum((fsdp_sums[7], fsdp_sums[8]), "dp")
-    shards = matrices + (gain_totals[0], gain_totals[1])
+    width = inputs.shape[-1]
+    rows = width // n_group
+    ff_part = w_down.shape[0]
+    bf = jnp.bfloat16
+    attn_block = jnp.concatenate([g.astype(bf) for g in grads[:4]], axis=1)
+    down_block = (
+        grads[6]
+        .astype(bf)
+        .reshape(n_group, rows, n_group, ff_part)
+        .transpose(2, 1, 0, 3)
+        .reshape(width, n_group * ff_part)
+    )
+    blocks = (attn_block, grads[4].astype(bf), grads[5].astype(bf), down_block)
+    totals = reduce_blocks(blocks, n_copies, n_group)
+    total_attn, total_gate, total_up, total_down = [
+        t.astype(jnp.float32) * scale for t in totals
+    ]
+    cut = [w_query.shape[1], key_weight.shape[1], value_weight.shape[1], w_output.shape[1]]
+    edges = [sum(cut[:k]) for k in range(5)]
+    total_down = (
+        total_down.reshape(rows, n_group, ff_part).transpose(2, 1, 0).reshape(ff_part, n_group, rows)
+    )
+    gain_totals = lax.psum(jnp.stack([grads[7], grads[8]]), ("dp", "fsdp"))
+    gain_shard = scale * lax.dynamic_slice_in_dim(
+        gain_totals, lax.axis_index("fsdp") * rows, rows, axis=1
+    )
     return (
         outputs,
         grad_inputs,
-        shards[0] * scale,
-        shards[1] * scale,
-        shards[2] * scale,
-        shards[3] * scale,
-        shards[4] * scale,
-        shards[5] * scale,
-        shards[6] * scale,
-        shards[7] * scale,
-        shards[8] * scale,
+        *(total_attn[:, edges[k] : edges[k + 1]] for k in range(4)),
+        total_gate,
+        total_up,
+        total_down.reshape(ff_part, width),
+        gain_shard[0],
+        gain_shard[1],
     )
 
 

time: 903 us -> 501 us (0.55)
  waiting for transfers between devices: 542 us -> 117 us
  Pallas kernels: 0 us -> 145 us
  blocking collectives: 182 us -> 67 us
  local copies, waits for them, and re-layouts: 68.7 us -> 81.8 us
  other arithmetic: 23 us -> 12 us
    reduce_scatter x7 -> x0, waiting for transfers between devices: 224 us -> none  [the longest x1 50 us: per_device(): lax.psum_scatter(grads[6].astype(jnp.bfloat16), 'fsdp', scatter_dimension...]
    unnamed x17 -> x5, waiting for transfers between devices: 179 us -> 3.11 us
    pallas_call x0 -> x1, Pallas kernels: none -> 145 us  [reduce_blocks(): pl.pallas_call(functools.partial(reduce_kernel, n_copies, n_group, n_bloc...]
    all_gather x4 -> x0, blocking collectives: 128 us -> none  [the longest x1 33.7 us: per_device(): lax.all_gather(pieces[3].astype(jnp.bfloat16), 'dp', axis=0, tiled=True)]
    all_gather x3 -> x0, waiting for transfers between devices: 27.3 us -> none  [the longest x1 27.3 us: per_device(): lax.all_gather(pieces[5].astype(jnp.bfloat16), 'dp', axis=0, tiled=True)]
    psum x1, blocking collectives: 19.9 us -> 39.2 us  [per_device(): gain_totals = lax.psum(jnp.stack([grads[7], grads[8]]), ('dp', 'fsdp'))]
    reshape x0 -> x2, local copies, waits for them, and re-layouts: none -> 17.7 us  [per_device(): down_block = grads[6].astype(bf).reshape(n_group, rows, n_group, ff_part)...]
    unnamed x131 -> x101, local copies, waits for them, and re-layouts: 33.1 us -> 15.7 us
  transfers between devices with their start and end apart: 16 -> 5, of which waited for: 12 -> 4; matrix products, arithmetic and copies ran while one was open for 13% -> 6% of each run, Pallas kernels for 0% -> 0%
where the time goes in v1:
time: 501 us; the launch traced here: 495 us
  Pallas kernels  145 us (29%)
  waiting for transfers between devices  117 us (23%)
  local copies, waits for them, and re-layouts  81.8 us (16%)
  blocking collectives  67 us (13%)
  matrix products  56.8 us (11%)
  between operations  15.5 us (3%)
  other arithmetic  12 us (2%)
    pallas_call x1, Pallas kernels, reduce_blocks(): pl.pallas_call(functools.partial(reduce_kernel, n_copies, n_group, n_bloc...  145 us
    psum x1, blocking collectives, per_device(): gain_totals = lax.psum(jnp.stack([grads[7], grads[8]]), ('dp', 'fsdp'))  39.2 us
    all_gather x1, waiting for transfers between devices, per_device(): lax.all_gather(w_up, 'fsdp', axis=0, tiled=True)  36.9 us
    all_gather x1, waiting for transfers between devices, per_device(): lax.all_gather(w_gate, 'fsdp', axis=0, tiled=True)  35.3 us
    all_gather x1, waiting for transfers between devices, per_device(): lax.all_gather(w_down, 'fsdp', axis=0, tiled=True)  35.3 us
    dot_general x7, matrix products, matrix_product(): jnp.dot(left_matrix, right_matrix, preferred_element_type=jnp.float32)  19.7 us
    reshape x2, local copies, waits for them, and re-layouts, per_device(): down_block = grads[6].astype(bf).reshape(n_group, rows, n_group, ff_part)...  17.7 us
    dot_general x7, matrix products, matmul_tn(): lax.dot_general(left_matrix, right_matrix, (((0,), (0,)), ((), ())), pref...  16.3 us
  transfers between devices with their start and end apart: 5, of which 4 were waited for; matrix products, arithmetic and copies ran while one was open for 6% of the time, Pallas kernels for 0%

profile of v1, /device:TPU:0, one launch (start us, length us, event | category | flops | bytes accessed | tf_op | source)
XLA Modules:
  0.0 494.9 jit_solution(12650653616850802145)
XLA Ops:
  7.3 0.7 all-gather.8.cloned.1.call-update
  8.0 0.7 all-gather.10.cloned.1.call-update
  8.8 0.7 all-gather.14.cloned.1.call-update
  10.6 0.6 dynamic-slice
  12.4 8.4 %all-reduce.2 = (bf16[960]{0:T(1024)(128)(2,1)S(1)}, bf16[960]{0:T(1024)(128)(2,1)S(1)}) all-reduce(bf16[960]{0:T(1024)(128)(2,1)S(1)} %dynamic-update-slice, bf16[960]{0:T(1024)(128)(2,1)S(1)} %dynamic-update-slice.1), channel_id=1, replica_groups=mesh['dp'=8,'fsdp'=4] {'fsdp'}, use_global_device_ids=true, to_apply=%add | all-reduce | flops 1920 | bytes 7680
  20.8 11.5 %all-gather.1 = bf16[4,240,320]{1,2,0:T(8,128)(2,1)S(1)} all-gather(bf16[1,240,320]{1,2,0:T(8,128)(2,1)S(1)} %bitcast.248), channel_id=1, replica_groups=mesh['dp'=8,'fsdp'=4] {'fsdp'}, dimensions={0}, use_global_device_ids=true | all-gather | bytes 768000 | tf_op jit(solution)/shard_map/all_gather | solution.py:562
  32.7 0.5 reshape.435
  33.3 8.0 %all-gather = bf16[4,240,320]{1,2,0:T(8,128)(2,1)S(1)} all-gather(bf16[1,240,320]{1,2,0:T(8,128)(2,1)S(1)} %bitcast.249), channel_id=1, replica_groups=mesh['dp'=8,'fsdp'=4] {'fsdp'}, dimensions={0}, use_global_device_ids=true | all-gather | bytes 768000 | tf_op jit(solution)/shard_map/all_gather | solution.py:563
  41.8 0.5 reshape.433
  42.9 0.8 copy.102
  43.7 0.6 iota_compare_fusion
  45.1 4.1 copy.104
  49.3 2.3 convolution_bitcast_fusion
  51.8 0.7 copy-done.31
  52.5 0.6 fusion.60
  53.5 1.3 convolution_convert_fusion.7
  54.8 6.3 %all-gather.10.cloned.1.call-done = bf16[960,960]{1,0:T(8,128)(2,1)} async-done(((bf16[240,960]{1,0:T(8,128)(2,1)}), bf16[960,960]{1,0:T(8,128)(2,1)}) %all-gather.10.cloned.1.call-update) | async-done | bytes 1843216 | tf_op jit(solution)/shard_map/all_gather | solution.py:564
  61.1 2.4 multiply_reduce_fusion
  63.5 0.9 fusion.27
  64.4 36.9 %all-gather.14.cloned.1.call-done = bf16[960,2560]{1,0:T(8,128)(2,1)} async-done(((bf16[240,2560]{1,0:T(8,128)(2,1)}), bf16[960,2560]{1,0:T(8,128)(2,1)}) %all-gather.14.cloned.1.call-update) | async-done | bytes 4915216 | tf_op jit(solution)/shard_map/all_gather | solution.py:566
  101.3 4.7 fusion.62
  106.0 35.3 %all-gather.12.cloned.1.call-done = bf16[960,2560]{1,0:T(8,128)(2,1)} async-done(((bf16[240,2560]{1,0:T(8,128)(2,1)}), bf16[960,2560]{1,0:T(8,128)(2,1)}) %all-gather.12.cloned.1.call-update) | async-done | bytes 4915216 | tf_op jit(solution)/shard_map/all_gather | solution.py:565
  141.3 4.7 fusion.61
  146.0 35.3 %all-gather.16.cloned.1.call-done = bf16[2560,960]{0,1:T(8,128)(2,1)} async-done(((bf16[640,960]{0,1:T(8,128)(2,1)}), bf16[2560,960]{0,1:T(8,128)(2,1)}) %all-gather.16.cloned.1.call-update) | async-done | bytes 4915216 | tf_op jit(solution)/shard_map/all_gather | solution.py:567
  181.2 5.9 %multiply_convert_fusion = (bf16[160,2560]{1,0:T(8,128)(2,1)S(1)}, bf16[160,2560]{1,0:T(8,128)(2,1)S(1)}, bf16[160,2560]{1,0:T(8,128)(2,1)}) fusion(f32[160,2560]{1,0:T(8,128)} %fusion.61, f32[160,2560]{1,0:T(8,128)} %fusion.62, bf16[2560,960]{0,1:T(8,128)(2,1)} %all-gather.16.cloned.1.call-done, bf16[1,160,960]{2,1,0:T(8,128)(2,1)} %param.12), kind=kOutput, calls=%fused_computation.21 | convolution fusion | flops 792985600 | bytes 10956800 | tf_op jit(solution)/shard_map/dot_general | solution.py:30
  187.1 1.6 fusion.63
  188.8 4.2 fusion.23
  193.3 0.8 copy-done.12
  194.1 1.9 convolution_convert_fusion.3
  196.0 1.5 convolution_convert_fusion.8
  197.5 2.0 copy.106
  199.5 1.6 fusion.11
  201.2 0.7 fusion.1
  201.9 0.6 fusion.9
  204.2 4.0 convolution_convert_fusion.1
  208.2 3.7 convolution_convert_fusion.2
  212.3 1.2 copy.111
  213.7 0.7 copy-done.27
  214.8 1.2 copy.110
  216.1 2.1 convolution_convert_fusion.4
  218.2 3.8 fusion
  221.9 9.3 %reshape.422 = bf16[4,240,4,640]{3,2,1,0:T(4,128)(2,1)} reshape(bf16[960,2560]{1,0:T(8,128)(2,1)} %fusion) | data formatting | bytes 9830400 | tf_op jit(solution)/shard_map/reshape | solution.py:584
  231.2 8.4 %copy.131 = bf16[4,240,4,640]{3,0,1,2:T(4,128)(2,1)} copy(bf16[4,240,4,640]{3,2,1,0:T(4,128)(2,1)} %reshape.422) | data formatting | bytes 9830400 | tf_op jit(solution)/shard_map/reshape | solution.py:584
  239.6 9.1 %reshape_reshape.4.refs_3_ = bf16[2,2,2,120,2560]{4,3,2,1,0:T(8,128)(2,1)} reshape(bf16[4,240,4,640]{3,2,1,0:T(4,128)(2,1)} %bitcast.217) | data formatting | bytes 9830400 | tf_op jit(solution)/shard_map/reshape;reshape | solution.py:539
  248.7 8.7 %concatenate.58 = bf16[960,2560]{1,0:T(8,128)(2,1)} concatenate(bf16[960,960]{1,0:T(8,128)(2,1)} %convolution_convert_fusion.4, bf16[960,320]{1,0:T(8,128)(2,1)} %copy.110, bf16[960,320]{1,0:T(8,128)(2,1)} %copy.111, bf16[960,960]{1,0:T(8,128)(2,1)S(1)} %copy-done.5), dimensions={1} | concatenate | bytes 9830400 | tf_op jit(solution)/shard_map/concatenate | solution.py:580
  257.4 144.8 %shard_map.194 = bf16[20,2,120,512]{3,2,1,0:T(8,128)(2,1)} custom-call(bf16[2,2,2,120,2560]{4,3,2,1,0:T(8,128)(2,1)} %bitcast.216, bf16[2,2,2,120,2560]{4,3,2,1,0:T(8,128)(2,1)} %bitcast.215, bf16[2,2,2,120,2560]{4,3,2,1,0:T(8,128)(2,1)} %bitcast.214, bf16[2,2,2,120,2560]{4,3,2,1,0:T(8,128)(2,1)} %reshape_reshape.4.refs_3_), custom_call_target="tpu_custom_call" | custom-call | tf_op jit(solution)/shard_map/pallas_call | solution.py:509
  402.2 6.1 %convert_multiply_fusion = (f32[5,2,120,512]{3,2,1,0:T(8,128)}, f32[5,2,120,512]{3,2,1,0:T(8,128)}, f32[5,2,120,512]{3,2,1,0:T(8,128)S(1)}, f32[5,2,120,512]{3,2,1,0:T(8,128)}) fusion(bf16[20,2,120,512]{3,2,1,0:T(8,128)(2,1)} %shard_map.194), kind=kLoop, calls=%fused_computation.12 | loop fusion | flops 4915200 | bytes 14745600 | tf_op jit(solution)/shard_map/mul | solution.py:591
  408.3 3.2 copy.113
  411.5 2.1 fusion.58
  413.6 3.0 fusion.57
  416.6 0.7 fusion.64
  418.0 1.3 fusion.21
  419.3 39.2 %psum.7 = f32[2,960]{1,0:T(2,128)S(1)} all-reduce(f32[2,960]{1,0:T(2,128)S(1)} %pad_maximum_fusion.3), channel_id=1, replica_groups=mesh['dp'=8,'fsdp'=4] {'dp','fsdp'}, use_global_device_ids=true, to_apply=%region_9.10 | all-reduce | flops 1920 | bytes 15360 | tf_op jit(solution)/shard_map/psum | solution.py:598
  458.6 0.6 fusion.59
  459.2 3.2 copy.115
  462.4 3.2 copy.121
  465.5 3.2 copy.116
  468.7 3.2 copy.117
  471.9 2.1 copy.114
  473.9 3.2 copy.120
  477.2 2.5 copy.119
  479.7 1.3 copy.118
  481.0 2.2 fusion.20
  483.2 4.8 fusion.10
  (128 shorter events, 8.5 us)
Async XLA Ops:
  7.2 3.4 copy-start.44
  7.2 4.7 copy-start.42
  7.2 4.9 copy-start.43
  7.2 13.5 %copy-start.39 = (bf16[240,320]{0,1:T(8,128)(2,1)S(1)}, bf16[240,320]{0,1:T(8,128)(2,1)}, u32[]{:S(2)}) copy-start(bf16[240,320]{0,1:T(8,128)(2,1)} %param.14) | copy-start | bytes 460804
  7.2 37.9 %all-gather.8.cloned.1.call-start = ((), (), s32[]{:S(2)}) async-start(), calls=%async_computation | async-start | bytes 2457600 | tf_op jit(solution)/shard_map/all_gather | solution.py:561
  8.0 53.2 %all-gather.10.cloned.1.call-start = ((), (), s32[]{:S(2)}) async-start(), calls=%async_computation.1 | async-start | bytes 2457600 | tf_op jit(solution)/shard_map/all_gather | solution.py:564
  8.7 92.6 %all-gather.14.cloned.1.call-start = ((), (), s32[]{:S(2)}) async-start(), calls=%async_computation.3 | async-start | bytes 6144000 | tf_op jit(solution)/shard_map/all_gather | solution.py:566
  9.4 131.8 %all-gather.12.cloned.1.call-start = ((), (), s32[]{:S(2)}) async-start(), calls=%async_computation.2 | async-start | bytes 6144000 | tf_op jit(solution)/shard_map/all_gather | solution.py:565
  10.0 23.3 %copy-start.40 = (bf16[240,320]{0,1:T(8,128)(2,1)S(1)}, bf16[240,320]{0,1:T(8,128)(2,1)}, u32[]{:S(2)}) copy-start(bf16[240,320]{0,1:T(8,128)(2,1)} %param.15) | copy-start | bytes 460804
  10.0 171.2 %all-gather.16.cloned.1.call-start = ((), (), s32[]{:S(2)}) async-start(), calls=%async_computation.4 | async-start | bytes 6144000 | tf_op jit(solution)/shard_map/all_gather | solution.py:567
  32.7 9.6 %copy-start.1 = (bf16[1,160,960]{2,1,0:T(8,128)(2,1)S(1)}, bf16[1,160,960]{2,1,0:T(8,128)(2,1)}, u32[]{:S(2)}) copy-start(bf16[1,160,960]{2,1,0:T(8,128)(2,1)} %param.11) | copy-start | bytes 921604
  33.3 11.1 %copy-start.19 = (bf16[960,320]{0,1:T(8,128)(2,1)}, bf16[960,320]{0,1:T(8,128)(2,1)S(1)}, u32[]{:S(2)}) copy-start(bf16[960,320]{0,1:T(8,128)(2,1)S(1)} %reshape.435) | copy-start | bytes 1843204
  42.4 6.9 %copy-start.21 = (bf16[960,320]{0,1:T(8,128)(2,1)}, bf16[960,320]{0,1:T(8,128)(2,1)S(1)}, u32[]{:S(2)}) copy-start(bf16[960,320]{0,1:T(8,128)(2,1)S(1)} %reshape.433) | copy-start | bytes 1843204
  45.1 6.7 %copy-start.35 = (bf16[160,5,32]{0,2,1:T(8,128)(2,1)}, bf16[160,5,32]{0,2,1:T(8,128)(2,1)S(1)}, u32[]{:S(2)}) copy-start(bf16[160,5,32]{0,2,1:T(8,128)(2,1)S(1)} %get-tuple-element.89) | copy-start | bytes 153604
  45.1 6.7 %copy-start.37 = (bf16[160,5,32]{0,2,1:T(8,128)(2,1)}, bf16[160,5,32]{0,2,1:T(8,128)(2,1)S(1)}, u32[]{:S(2)}) copy-start(bf16[160,5,32]{0,2,1:T(8,128)(2,1)S(1)} %get-tuple-element.90) | copy-start | bytes 153604
  49.3 3.2 copy-start.41
  51.8 0.7 copy-start.31
  51.8 1.3 copy-start.33
  52.5 1.1 copy-start.23
  181.2 5.9 %copy-start = (bf16[960,2560]{1,0:T(8,128)(2,1)S(1)}, bf16[960,2560]{1,0:T(8,128)(2,1)}, u32[]{:S(2)}) copy-start(bf16[960,2560]{1,0:T(8,128)(2,1)} %all-gather.12.cloned.1.call-done) | copy-start | bytes 14745604
  187.1 1.7 copy-start.15
  187.1 1.7 copy-start.17
  188.8 4.3 copy-start.29
  193.0 1.0 copy-start.12
  193.1 2.9 copy-start.7
  194.1 1.9 copy-start.3
  199.5 1.7 copy-start.13
  199.5 1.7 copy-start.24
  201.2 10.7 %copy-start.25 = (bf16[5,64,160]{2,1,0:T(8,128)(2,1)}, bf16[5,64,160]{2,1,0:T(8,128)(2,1)S(1)}, u32[]{:S(2)}) copy-start(bf16[5,64,160]{2,1,0:T(8,128)(2,1)S(1)} %fusion.11) | copy-start | bytes 307204
  201.8 0.9 copy-start.32
  201.9 1.1 copy-start.34
  201.9 1.6 copy-start.36
  201.9 1.6 copy-start.38
  202.9 1.0 copy-start.2
  202.9 1.3 copy-start.18
  204.2 4.0 copy-start.16
  213.7 0.7 copy-start.27
  214.8 3.4 copy-start.8
  214.8 3.4 copy-start.30
  216.1 5.9 %copy-start.10 = (bf16[1,160,15,64]{1,3,2,0:T(8,128)(2,1)}, bf16[1,160,15,64]{1,3,2,0:T(8,128)(2,1)S(1)}, u32[]{:S(2)}) copy-start(bf16[1,160,15,64]{1,3,2,0:T(8,128)(2,1)S(1)} %maximum_convert_fusion) | copy-start | bytes 921604
  239.6 9.1 %copy-start.5 = (bf16[960,960]{1,0:T(8,128)(2,1)S(1)}, bf16[960,960]{1,0:T(8,128)(2,1)}, u32[]{:S(2)}) copy-start(bf16[960,960]{1,0:T(8,128)(2,1)} %convolution_convert_fusion.3) | copy-start | bytes 5529604
  411.5 5.1 %copy-start.6 = (bf16[960,960]{1,0:T(8,128)(2,1)S(1)}, bf16[960,960]{1,0:T(8,128)(2,1)}, u32[]{:S(2)}) copy-start(bf16[960,960]{1,0:T(8,128)(2,1)} %all-gather.8.cloned.1.call-done) | copy-start | bytes 5529604
  411.5 5.1 %copy-start.11 = (bf16[1,160,15,64]{1,3,2,0:T(8,128)(2,1)S(1)}, bf16[1,160,15,64]{1,3,2,0:T(8,128)(2,1)}, u32[]{:S(2)}) copy-start(bf16[1,160,15,64]{1,3,2,0:T(8,128)(2,1)} %copy-done.10) | copy-start | bytes 921604
  416.5 1.1 copy-start.20
  416.5 1.1 copy-start.28
  416.5 1.5 copy-start.22
  416.6 1.5 copy-start.26
  473.9 5.8 %copy-start.14 = (f32[240,960]{0,1:T(8,128)S(1)}, f32[240,960]{0,1:T(8,128)}, u32[]{:S(2)}) copy-start(f32[240,960]{0,1:T(8,128)} %get-tuple-element.80) | copy-start | bytes 2764804
  477.2 3.8 copy-start.4
  479.7 3.5 copy-start.9
Sparse Core Ops, SparseCore 0:
  9.6 28.0 all-gather.7
  39.2 21.8 all-gather.9
  62.7 38.5 all-gather.13
  102.7 38.5 all-gather.11
  142.7 38.4 all-gather.15

commit v2 on v1

--- a/solution.py
+++ b/solution.py
@@ -266,15 +266,16 @@
     return n_copies // outer, outer
 
 
-def reduce_kernel(n_copies, n_group, n_blocks, per_block, *refs):
-    sources = refs[:n_blocks]
-    out_hbm = refs[n_blocks]
-    own, from_core, from_pair, from_inner, from_outer, final = refs[n_blocks + 1 : n_blocks + 7]
+def reduce_kernel(n_copies, n_group, per_block, down_direct, *refs):
+    sources = refs[:5]
+    out_hbm, out_down, out_gain = refs[5:8]
+    own, from_core, from_pair, from_inner, from_outer, final = refs[8:14]
     (load_sem, store_sem, send_core, recv_core, send_pair, recv_pair, send_in, recv_in,
-     send_out, recv_out, send_ago, recv_ago, send_agi, recv_agi) = refs[n_blocks + 7 :]
+     send_out, recv_out, send_ago, recv_ago, send_agi, recv_agi) = refs[14:]
     inner_n, outer_n = dp_split(n_copies)
     pair_n = n_group // 2
-    steps = n_blocks * per_block
+    steps = 4 * per_block + 1
+    down_start = 3 * per_block
     copy_id = lax.axis_index("dp")
     member = lax.axis_index("fsdp")
     pair, core = member // 2, member % 2
@@ -398,12 +399,59 @@
             (outer * inner_n + inner_peer(k), member),
         )
 
-    def store_copy(t):
-        return pltpu.make_async_copy(final.at[t], out_hbm.at[t], store_sem.at[t])
-
+    def store_copy(t, target):
+        return pltpu.make_async_copy(final.at[t], target, store_sem.at[t])
+
+    def start_store(t):
+        @pl.when(t < down_start)
+        def _():
+            cols = pl.ds(pl.multiple_of(lax.rem(t, per_block) * CHUNK, CHUNK), CHUNK)
+            store_copy(t, out_hbm.at[t // per_block, :, :, cols]).start()
+
+        @pl.when((t >= down_start) & (t < steps - 1))
+        def _():
+            c = t - down_start
+            if down_direct:
+                cols = pl.ds(pl.multiple_of(c * tile, tile), tile)
+                for b in range(n_group):
+                    pltpu.make_async_copy(
+                        final.at[t, :, :, pl.ds(b * tile, tile)],
+                        out_down.at[b, :, :, cols],
+                        store_sem.at[t],
+                    ).start()
+            else:
+                cols = pl.ds(pl.multiple_of(c * CHUNK, CHUNK), CHUNK)
+                store_copy(t, out_down.at[:, :, cols]).start()
+
+        @pl.when(t == steps - 1)
+        def _():
+            store_copy(t, out_gain).start()
+
+    tile = CHUNK // n_group
+    part_width = sources[3].shape[-1] // n_group
     for t in range(steps):
-        core_copy(t, sources[t // per_block], t % per_block).start()
-        load_copy(t, sources[t // per_block], t % per_block).start()
+        block, c = t // per_block, t % per_block
+        if block == 3 and down_direct:
+            for p in range(pair_n):
+                for b in range(n_group):
+                    place = (slice(None), slice(None), pl.ds(b * tile, tile))
+                    theirs = pl.multiple_of((p * 2 + 1 - core) * part_width + c * tile, tile)
+                    mine = pl.multiple_of((p * 2 + core) * part_width + c * tile, tile)
+                    remote(
+                        sources[3].at[b, :, :, pl.ds(theirs, tile)],
+                        from_core.at[(t, p) + place],
+                        send_core.at[t],
+                        recv_core.at[t],
+                        core_device,
+                    ).start()
+                    pltpu.make_async_copy(
+                        sources[3].at[b, :, :, pl.ds(mine, tile)],
+                        own.at[(t, p) + place],
+                        load_sem.at[t],
+                    ).start()
+        else:
+            core_copy(t, sources[block], c).start()
+            load_copy(t, sources[block], c).start()
 
     def stage_core(t):
         core_copy(t, sources[0], 0).wait_recv()
@@ -461,7 +509,7 @@
     def stage_store(t):
         for k in range(1, inner_n):
             landed_inner(t, k).wait_recv()
-        store_copy(t).start()
+        start_store(t)
 
     lags = ((stage_core, 0), (stage_pair, 4), (stage_inner, 6), (stage_outer, 8),
             (stage_spread, 10), (stage_store, 12))
@@ -485,20 +533,21 @@
         for k in range(1, outer_n):
             outer_copy(t, k).wait_send()
             spread_outer(t, k).wait_send()
-        store_copy(t).wait()
+        store_copy(t, out_gain).wait()
         return carry
 
     lax.fori_loop(0, steps, drain, 0)
 
 
-def reduce_blocks(blocks, n_copies, n_group):
-    n_blocks = len(blocks)
+def reduce_blocks(blocks, down, gains, n_copies, n_group):
     total_rows, total_columns = blocks[0].shape
     inner_n, outer_n = dp_split(n_copies)
     pair_n = n_group // 2
     part = total_rows // (n_group * inner_n)
     per_block = total_columns // CHUNK
-    steps = n_blocks * per_block
+    steps = 4 * per_block + 1
+    part_width = total_columns // n_group
+    down_direct = n_group * 128 == CHUNK and part_width % 128 == 0
     piece = CHUNK // outer_n
     bf = jnp.bfloat16
     dma = pltpu.SemaphoreType.DMA
@@ -506,11 +555,31 @@
     def many(n):
         return dma((steps, max(n - 1, 1)))
 
-    gathered = pl.pallas_call(
-        functools.partial(reduce_kernel, n_copies, n_group, n_blocks, per_block),
-        out_shape=jax.ShapeDtypeStruct((steps, inner_n, part, CHUNK), bf),
-        in_specs=[pl.BlockSpec(memory_space=pl.ANY)] * n_blocks,
-        out_specs=pl.BlockSpec(memory_space=pl.ANY),
+    grouped = (pair_n, 2, inner_n, part)
+    if down_direct:
+        down = down.reshape(n_group, inner_n, part, total_columns)
+        down_shape = (n_group, inner_n, part, part_width)
+    else:
+        down = (
+            down.reshape(n_group, total_rows // n_group, n_group, part_width)
+            .transpose(2, 1, 0, 3)
+            .reshape(*grouped, total_columns)
+        )
+        down_shape = (inner_n, part, total_columns)
+    gain_width = gains.shape[-1]
+    gains = (
+        jnp.pad(gains, ((0, 0), (0, inner_n * part * CHUNK - gain_width)))
+        .reshape(*grouped, CHUNK)
+    )
+    big, down_sum, gain_sum = pl.pallas_call(
+        functools.partial(reduce_kernel, n_copies, n_group, per_block, down_direct),
+        out_shape=[
+            jax.ShapeDtypeStruct((3, inner_n, part, total_columns), bf),
+            jax.ShapeDtypeStruct(down_shape, bf),
+            jax.ShapeDtypeStruct((inner_n, part, CHUNK), bf),
+        ],
+        in_specs=[pl.BlockSpec(memory_space=pl.ANY)] * 5,
+        out_specs=[pl.BlockSpec(memory_space=pl.ANY)] * 3,
         scratch_shapes=[
             pltpu.VMEM((steps, pair_n, inner_n, part, CHUNK), bf),
             pltpu.VMEM((steps, pair_n, inner_n, part, CHUNK), bf),
@@ -536,12 +605,200 @@
         compiler_params=pltpu.CompilerParams(
             collective_id=0, has_side_effects=True, vmem_limit_bytes=60 * 1024 * 1024
         ),
-    )(*(b.reshape(pair_n, 2, inner_n, part, total_columns) for b in blocks))
-    gathered = gathered.reshape(n_blocks, per_block, inner_n * part, CHUNK)
-    return [
-        gathered[b].transpose(1, 0, 2).reshape(inner_n * part, total_columns)
-        for b in range(n_blocks)
-    ]
+    )(*(b.reshape(*grouped, total_columns) for b in blocks), down, gains)
+    rows = inner_n * part
+    big = big.reshape(3, rows, total_columns)
+    if down_direct:
+        down_sum = down_sum.reshape(total_rows, part_width)
+    else:
+        down_sum = (
+            down_sum.reshape(rows, n_group, part_width).transpose(1, 0, 2).reshape(total_rows, part_width)
+        )
+    return big, down_sum, gain_sum.reshape(-1)[:gain_width]
+
+
+def gather_kernel(n_copies, n_group, *refs):
+    shards = refs[:5]
+    outs = refs[5:10]
+    (own_sem, core_send, core_recv, pair_send, pair_recv, in_send, in_recv, out_send, out_recv,
+     diag_send, diag_recv, piece_send, piece_recv, gain_send, gain_recv) = refs[10:]
+    inner_n, outer_n = dp_split(n_copies)
+    pair_n = n_group // 2
+    copy_id = lax.axis_index("dp")
+    member = lax.axis_index("fsdp")
+    pair, core = member // 2, member % 2
+    outer, inner = copy_id // inner_n, copy_id % inner_n
+    a_bit, b_bit = inner % 2, outer % 2
+    a_device = (outer * inner_n + inner + 1 - 2 * a_bit, member)
+    b_device = ((outer + 1 - 2 * b_bit) * inner_n + inner, member)
+    core_device = (copy_id, pair * 2 + 1 - core)
+
+    def peer(k):
+        return (copy_id, ((pair + k) % pair_n) * 2 + core)
+
+    devices = [core_device, a_device, b_device]
+    devices += [peer(k) for k in range(1, pair_n)]
+    devices += [(copy_id, ((pair + k) % pair_n) * 2 + 1 - core) for k in range(1, pair_n)]
+    barrier = pltpu.get_barrier_semaphore()
+    for device in devices:
+        pl.semaphore_signal(
+            barrier, inc=1, device_id=device, device_id_type=pl.DeviceIdType.MESH
+        )
+    pl.semaphore_wait(barrier, len(devices))
+
+    def remote(src, dst, send, recv, device):
+        return pltpu.make_async_remote_copy(
+            src_ref=src,
+            dst_ref=dst,
+            send_sem=send,
+            recv_sem=recv,
+            device_id=device,
+            device_id_type=pl.DeviceIdType.MESH,
+        )
+
+    def cut(ref, w, q):
+        rows, columns = shards[w].shape
+        if w < 3:
+            size = columns // 4
+            return ref.at[:, pl.ds(pl.multiple_of(q * size, size), size)]
+        size = rows // 4
+        return ref.at[pl.ds(pl.multiple_of(q * size, size), size), :]
+
+    def index(a, b):
+        return a * 2 + b
+
+    pieces = (
+        index(a_bit, b_bit),
+        index(1 - a_bit, b_bit),
+        index(a_bit, 1 - b_bit),
+        index(1 - a_bit, 1 - b_bit),
+    )
+    route = ("a", "b", "y", "y")
+    pending = []
+
+    def launch(copy):
+        copy.start()
+        pending.append(copy)
+
+    def source(k):
+        return ((pair + pair_n - k) % pair_n) * 2 + core
+
+    def arrived(w, k, kind, send, recv):
+        place = cut(outs[w].at[source(k)], w, pieces[kind])
+        return remote(place, place, send.at[w, k - 1], recv.at[w, k - 1], core_device)
+
+    def pass_on(w, k, kind, send, recv, device):
+        place = cut(outs[w].at[source(k)], w, pieces[kind])
+        launch(remote(place, place, send.at[w, k - 1], recv.at[w, k - 1], device))
+
+    def to_core(w, k, kind):
+        place = cut(outs[w].at[source(k)], w, pieces[kind])
+        launch(
+            remote(
+                place, place, piece_send.at[w, k - 1, kind], piece_recv.at[w, k - 1, kind],
+                core_device,
+            )
+        )
+
+    gain_peers = [core_device]
+    gain_peers += [(copy_id, ((pair + k) % pair_n) * 2 + core) for k in range(1, pair_n)]
+    gain_peers += [(copy_id, ((pair + k) % pair_n) * 2 + 1 - core) for k in range(1, pair_n)]
+    for k, device in enumerate(gain_peers):
+        launch(remote(shards[4], outs[4].at[member], gain_send.at[k], gain_recv.at[k], device))
+    for w in range(4):
+        for k in range(1, pair_n):
+            launch(
+                remote(
+                    cut(shards[w], w, pieces[0]),
+                    cut(outs[w].at[member], w, pieces[0]),
+                    pair_send.at[w, k - 1],
+                    pair_recv.at[w, k - 1],
+                    peer(k),
+                )
+            )
+    for w in range(4):
+        if route[w] == "y":
+            for k in range(1, pair_n):
+                launch(
+                    remote(
+                        cut(shards[w], w, pieces[3]),
+                        cut(outs[w].at[member], w, pieces[3]),
+                        diag_send.at[w, k - 1],
+                        diag_recv.at[w, k - 1],
+                        peer(k),
+                    )
+                )
+    locals_ = []
+    for w in range(4):
+        launch(remote(shards[w], outs[w].at[member], core_send.at[w], core_recv.at[w], core_device))
+    for w in range(5):
+        copy = pltpu.make_async_copy(shards[w], outs[w].at[member], own_sem.at[w])
+        copy.start()
+        locals_.append(copy)
+    for w in range(4):
+        for k in range(1, pair_n):
+            arrived(w, k, 0, pair_send, pair_recv).wait_recv()
+            pass_on(w, k, 0, in_send, in_recv, a_device)
+            pass_on(w, k, 0, out_send, out_recv, b_device)
+            to_core(w, k, 0)
+    for w in range(4):
+        for k in range(1, pair_n):
+            arrived(w, k, 1, in_send, in_recv).wait_recv()
+            if route[w] == "b":
+                pass_on(w, k, 1, diag_send, diag_recv, b_device)
+            to_core(w, k, 1)
+            arrived(w, k, 2, out_send, out_recv).wait_recv()
+            if route[w] == "a":
+                pass_on(w, k, 2, diag_send, diag_recv, a_device)
+            to_core(w, k, 2)
+    for w in range(4):
+        for k in range(1, pair_n):
+            arrived(w, k, 3, diag_send, diag_recv).wait_recv()
+            to_core(w, k, 3)
+    for w in range(4):
+        place = outs[w].at[pair * 2 + 1 - core]
+        remote(place, place, core_send.at[w], core_recv.at[w], core_device).wait_recv()
+        for k in range(1, pair_n):
+            other = ((pair + pair_n - k) % pair_n) * 2 + 1 - core
+            for kind in range(4):
+                place = cut(outs[w].at[other], w, pieces[kind])
+                remote(
+                    place, place, piece_send.at[w, k - 1, kind], piece_recv.at[w, k - 1, kind],
+                    core_device,
+                ).wait_recv()
+    for k in range(len(gain_peers)):
+        remote(
+            shards[4], outs[4].at[member], gain_send.at[k], gain_recv.at[k], core_device
+        ).wait_recv()
+    for copy in pending:
+        copy.wait_send()
+    for copy in locals_:
+        copy.wait()
+
+
+def gather_weights(shards, n_copies, n_group):
+    pair_n = n_group // 2
+    others = max(pair_n - 1, 1)
+    dma = pltpu.SemaphoreType.DMA
+    return pl.pallas_call(
+        functools.partial(gather_kernel, n_copies, n_group),
+        out_shape=[jax.ShapeDtypeStruct((n_group,) + w.shape, w.dtype) for w in shards],
+        in_specs=[pl.BlockSpec(memory_space=pltpu.VMEM)] * 5,
+        out_specs=[pl.BlockSpec(memory_space=pl.ANY)] * 5,
+        scratch_shapes=[
+            dma((5,)),
+            dma((4,)),
+            dma((4,)),
+            *[dma((4, others)) for _ in range(8)],
+            dma((4, others, 4)),
+            dma((4, others, 4)),
+            dma((n_group - 1,)),
+            dma((n_group - 1,)),
+        ],
+        compiler_params=pltpu.CompilerParams(
+            collective_id=1, has_side_effects=True, vmem_limit_bytes=40 * 1024 * 1024
+        ),
+    )(*shards)
 
 
 def per_device(
@@ -557,57 +814,67 @@
     attn_gain,
     mlp_gain,
 ):
+    n_copies = lax.axis_size("dp")
+    n_group = lax.axis_size("fsdp")
+    width = inputs.shape[-1]
+    rows = width // n_group
+    attn_shard = jnp.concatenate([w_query, key_weight, w_output, value_weight], axis=1)
+    gain_flat = jnp.concatenate([attn_gain, mlp_gain])
+    gain_lines = -(-gain_flat.shape[0] // 2048) * 16
+    gain_shard = jnp.pad(gain_flat, (0, gain_lines * 128 - gain_flat.shape[0]))
+    full_attn, full_gate, full_up, full_down, full_gain = gather_weights(
+        (attn_shard, w_gate, w_up, w_down, gain_shard.reshape(gain_lines, 128)),
+        n_copies,
+        n_group,
+    )
+    full_attn = full_attn.reshape(width, -1)
+    full_gain = full_gain.reshape(n_group, -1)
+    cut = [w_query.shape[1], key_weight.shape[1], w_output.shape[1], value_weight.shape[1]]
+    edges = [sum(cut[:k]) for k in range(5)]
     gathered = (
-        lax.all_gather(w_query, "fsdp", axis=0, tiled=True),
-        lax.all_gather(key_weight, "fsdp", axis=0, tiled=True),
-        lax.all_gather(value_weight, "fsdp", axis=0, tiled=True),
-        lax.all_gather(w_output, "fsdp", axis=0, tiled=True),
-        lax.all_gather(w_gate, "fsdp", axis=0, tiled=True),
-        lax.all_gather(w_up, "fsdp", axis=0, tiled=True),
-        lax.all_gather(w_down, "fsdp", axis=0, tiled=True),
-        lax.all_gather(attn_gain, "fsdp", axis=0, tiled=True),
-        lax.all_gather(mlp_gain, "fsdp", axis=0, tiled=True),
+        full_attn[:, edges[0] : edges[1]],
+        full_attn[:, edges[1] : edges[2]],
+        full_attn[:, edges[3] : edges[4]],
+        full_attn[:, edges[2] : edges[3]],
+        full_gate.reshape(width, -1),
+        full_up.reshape(width, -1),
+        full_down.reshape(-1, width),
+        full_gain[:, :rows].reshape(width),
+        full_gain[:, rows : 2 * rows].reshape(width),
     )
     outputs, saved = forward_pass(inputs, gathered)
     grad_inputs, grads = backward_pass(cotangent, gathered, saved)
-    n_copies = lax.axis_size("dp")
-    n_group = lax.axis_size("fsdp")
     scale = float(n_copies * n_group * inputs.shape[0] * inputs.shape[1]) ** (-0.5)
-    width = inputs.shape[-1]
-    rows = width // n_group
-    ff_part = w_down.shape[0]
     bf = jnp.bfloat16
-    attn_block = jnp.concatenate([g.astype(bf) for g in grads[:4]], axis=1)
-    down_block = (
-        grads[6]
-        .astype(bf)
-        .reshape(n_group, rows, n_group, ff_part)
-        .transpose(2, 1, 0, 3)
-        .reshape(width, n_group * ff_part)
-    )
-    blocks = (attn_block, grads[4].astype(bf), grads[5].astype(bf), down_block)
-    totals = reduce_blocks(blocks, n_copies, n_group)
-    total_attn, total_gate, total_up, total_down = [
-        t.astype(jnp.float32) * scale for t in totals
-    ]
-    cut = [w_query.shape[1], key_weight.shape[1], value_weight.shape[1], w_output.shape[1]]
-    edges = [sum(cut[:k]) for k in range(5)]
-    total_down = (
-        total_down.reshape(rows, n_group, ff_part).transpose(2, 1, 0).reshape(ff_part, n_group, rows)
-    )
-    gain_totals = lax.psum(jnp.stack([grads[7], grads[8]]), ("dp", "fsdp"))
-    gain_shard = scale * lax.dynamic_slice_in_dim(
-        gain_totals, lax.axis_index("fsdp") * rows, rows, axis=1
-    )
+    attn_block = jnp.concatenate(
+        [g.astype(bf) for g in (grads[0], grads[1], grads[3], grads[2])], axis=1
+    )
+    gain_block = jnp.concatenate(
+        [g.astype(bf).reshape(n_group, rows) for g in (grads[7], grads[8])], axis=1
+    )
+    big, down_sum, gain_sum = reduce_blocks(
+        (attn_block, grads[4].astype(bf), grads[5].astype(bf)),
+        grads[6].astype(bf),
+        gain_block,
+        n_copies,
+        n_group,
+    )
+
+    def scaled(value):
+        return value.astype(jnp.float32) * scale
+
     return (
         outputs,
         grad_inputs,
-        *(total_attn[:, edges[k] : edges[k + 1]] for k in range(4)),
-        total_gate,
-        total_up,
-        total_down.reshape(ff_part, width),
-        gain_shard[0],
-        gain_shard[1],
+        scaled(big[0, :, edges[0] : edges[1]]),
+        scaled(big[0, :, edges[1] : edges[2]]),
+        scaled(big[0, :, edges[3] : edges[4]]),
+        scaled(big[0, :, edges[2] : edges[3]]),
+        scaled(big[1]),
+        scaled(big[2]),
+        scaled(down_sum.T),
+        scaled(gain_sum[:rows]),
+        scaled(gain_sum[rows:]),
     )
 
 

time: 501 us -> 302 us (0.60)
  waiting for transfers between devices: 117 us -> 0 us
  blocking collectives: 67 us -> 0 us
  Pallas kernels: 145 us -> 201 us
  local copies, waits for them, and re-layouts: 81.8 us -> 38.1 us
  between operations: 15.5 us -> 1.25 us
  matrix products: 56.8 us -> 45.3 us
    all_gather x5 -> x0, waiting for transfers between devices: 114 us -> none  [the longest x1 36.9 us: per_device(): lax.all_gather(w_up, 'fsdp', axis=0, tiled=True)]
    pallas_call x1 -> x2, Pallas kernels: 145 us -> 201 us  [the longest x1 150 us: reduce_blocks(): pl.pallas_call(functools.partial(reduce_kernel, n_copies, n_group, per_bl...]
    psum x1 -> x0, blocking collectives: 39.2 us -> none  [per_device(): gain_totals = lax.psum(jnp.stack([grads[7], grads[8]]), ('dp', 'fsdp'))]
    all_gather x2 -> x0, blocking collectives: 19.5 us -> none  [the longest x1 11.5 us: per_device(): lax.all_gather(key_weight, 'fsdp', axis=0, tiled=True)]
    reshape x2 -> x0, local copies, waits for them, and re-layouts: 17.7 us -> none  [per_device(): down_block = grads[6].astype(bf).reshape(n_group, rows, n_group, ff_part)...]
    mul x4 -> x0, local copies, waits for them, and re-layouts: 11.6 us -> none  [per_device(): t.astype(jnp.float32) * scale]
    another operation x1 -> x0, local copies, waits for them, and re-layouts: 9.09 us -> none  [reduce_blocks(): b.reshape(pair_n, 2, inner_n, part, total_columns)]
    dot_general x7, matrix products: 19.7 us -> 11.1 us  [matrix_product(): jnp.dot(left_matrix, right_matrix, preferred_element_type=jnp.float32)]
  transfers between devices with their start and end apart: 5 -> 0, of which waited for: 4 -> 0; matrix products, arithmetic and copies ran while one was open for 6% -> 0% of each run, Pallas kernels for 0% -> 0%
where the time goes in v2:
time: 302 us; the launch traced here: 301 us
  Pallas kernels  201 us (67%)
  matrix products  45.3 us (15%)
  local copies, waits for them, and re-layouts  38.1 us (13%)
  other arithmetic  15.3 us (5%)
    pallas_call x1, Pallas kernels, reduce_blocks(): pl.pallas_call(functools.partial(reduce_kernel, n_copies, n_group, per_bl...  150 us
    pallas_call x1, Pallas kernels, gather_weights(): pl.pallas_call(functools.partial(gather_kernel, n_copies, n_group), out_s...  50.6 us
    dot_general x7, matrix products, matmul_tn(): lax.dot_general(left_matrix, right_matrix, (((0,), (0,)), ((), ())), pref...  18.2 us
    unnamed x82, local copies, waits for them, and re-layouts  14.4 us
    dot_general x7, matrix products, matmul_nt(): lax.dot_general(left_matrix, right_matrix, (((1,), (1,)), ((), ())), pref...  11.7 us
    dot_general x7, matrix products, matrix_product(): jnp.dot(left_matrix, right_matrix, preferred_element_type=jnp.float32)  11.1 us
    concatenate x1, local copies, waits for them, and re-layouts, per_device(): jnp.concatenate([g.astype(bf) for g in (grads[0], grads[1], grads[3], gra...  8.35 us
    mul x5, other arithmetic, scaled(): return value.astype(jnp.float32) * scale  7.63 us

profile of v2, /device:TPU:0, one launch (start us, length us, event | category | flops | bytes accessed | tf_op | source)
XLA Modules:
  0.0 300.9 jit_solution(7948063857255803114)
XLA Ops:
  0.7 1.1 fusion.38
  1.8 0.8 fusion.69.refs_4_
  2.5 0.6 iota_compare_fusion.1
  3.4 1.1 copy.52
  4.5 1.1 copy.53
  5.5 2.3 concatenate.59.refs_0_
  7.8 1.6 copy.54.refs_3_
  9.5 1.3 copy-done.1
  10.8 1.3 copy-done.2
  12.0 50.6 %shard_map.194 = (bf16[4,240,2560]{2,1,0:T(8,128)(2,1)S(1)}, bf16[4,240,2560]{2,1,0:T(8,128)(2,1)}, bf16[4,240,2560]{2,1,0:T(8,128)(2,1)}, bf16[4,640,960]{2,1,0:T(8,128)(2,1)}, bf16[4,16,128]{2,1,0:T(8,128)(2,1)S(1)}) custom-call(bf16[240,2560]{1,0:T(8,128)(2,1)S(1)} %concatenate.59.refs_0_, bf16[240,2560]{1,0:T(8,128)(2,1)S(1)} %copy-done.1, ...), custom_call_target="tpu_custom_call" | custom-call | tf_op jit(solution)/shard_map/pallas_call | solution.py:783
  62.7 2.2 copy-done
  65.2 1.6 convolution_convert_fusion.8
  66.9 1.5 slice_bitcast_fusion.1
  68.4 0.3 copy.56
  68.7 0.4 convolution_bitcast_fusion.3
  69.2 1.8 slice_bitcast_fusion
  71.0 2.4 copy.57
  73.4 2.3 convolution_bitcast_fusion.1
  75.9 0.6 fusion.80
  76.6 0.4 exponential_reduce_fusion
  77.1 0.5 convolution_convert_fusion.7
  77.6 2.9 multiply_reduce_fusion
  80.7 1.0 fusion.82
  81.7 0.3 slice-done.5
  82.0 1.0 fusion.81
  83.0 0.3 slice-done.6
  83.6 2.3 multiply_convert_fusion
  86.0 1.8 fusion.22
  87.8 1.6 fusion.83
  89.5 2.5 fusion.39
  92.1 1.6 fusion.42
  93.7 0.8 copy-done.6
  94.5 3.1 %fusion.23 = bf16[160,960]{1,0:T(8,128)(2,1)} fusion(bf16[960,2560]{1,0:T(8,128)(2,1)} %bitcast.212, f32[1,160,960]{2,1,0:T(8,128)S(1)} %fusion.42), kind=kOutput, calls=%fused_computation.47 | convolution fusion | flops 295219200 | bytes 2887680 | tf_op jit(solution)/shard_map/dot_general | solution.py:30
  97.6 2.0 copy.59
  99.6 1.6 fusion.26
  101.2 1.3 convolution_convert_fusion.5
  102.4 2.3 copy.64
  104.7 3.2 %convolution_convert_fusion.3 = bf16[960,960]{1,0:T(8,128)(2,1)} fusion(bf16[160,960]{0,1:T(8,128)(2,1)} %bitcast.249, f32[1,160,960]{2,1,0:T(8,128)} %copy-done.6), kind=kOutput, calls=%fused_computation.20 | convolution fusion | flops 295987200 | bytes 2764800 | tf_op jit(solution)/shard_map/dot_general | solution.py:24
  107.9 0.7 fusion
  108.6 0.8 fusion.21
  109.6 0.5 convolution_bitcast_fusion.5
  110.2 0.3 fusion.61
  110.9 1.0 slice-done.1
  111.9 0.7 fusion.11
  112.7 0.6 convolution_add_fusion.1
  113.3 0.8 fusion.37
  114.2 1.1 fusion.36
  115.3 0.4 convolution_convert_fusion.6
  115.7 1.2 copy.63
  116.9 0.3 fusion.27
  117.2 1.1 copy.78
  118.3 2.1 convolution_convert_fusion.4
  120.4 8.3 %concatenate.69 = bf16[960,2560]{1,0:T(8,128)(2,1)} concatenate(bf16[960,960]{1,0:T(8,128)(2,1)} %convolution_convert_fusion.4, bf16[960,320]{1,0:T(8,128)(2,1)} %copy.63, bf16[960,960]{1,0:T(8,128)(2,1)S(1)} %copy-done.5, bf16[960,320]{1,0:T(8,128)(2,1)} %copy.64), dimensions={1} | concatenate | bytes 9830400 | tf_op jit(solution)/shard_map/concatenate | solution.py:849
  128.8 3.7 %convolution_convert_fusion = bf16[2560,960]{0,1:T(8,128)(2,1)} fusion(bf16[160,2560]{1,0:T(8,128)(2,1)S(1)} %copy-done.9, bf16[1,160,960]{2,1,0:T(8,128)(2,1)S(1)} %copy-done.18), kind=kOutput, calls=%fused_computation | convolution fusion | flops 788889600 | bytes 6041600 | tf_op jit(solution)/shard_map/dot_general | solution.py:24
  132.5 3.8 %convolution_convert_fusion.1 = bf16[960,2560]{1,0:T(8,128)(2,1)} fusion(bf16[160,960]{1,0:T(8,128)(2,1)S(1)} %fusion.46, bf16[160,2560]{1,0:T(8,128)(2,1)S(1)} %copy-done.15), kind=kOutput, calls=%fused_computation.1 | convolution fusion | flops 788889600 | bytes 6041600 | tf_op jit(solution)/shard_map/dot_general | solution.py:24
  136.3 3.7 %convolution_convert_fusion.2 = bf16[960,2560]{1,0:T(8,128)(2,1)} fusion(bf16[160,960]{1,0:T(8,128)(2,1)S(1)} %fusion.46, bf16[160,2560]{1,0:T(8,128)(2,1)S(1)} %copy-done.13), kind=kOutput, calls=%fused_computation.2 | convolution fusion | flops 788889600 | bytes 6041600 | tf_op jit(solution)/shard_map/dot_general | solution.py:24
  140.0 150.4 %shard_map.195 = (bf16[3,2,120,2560]{3,2,1,0:T(8,128)(2,1)}, bf16[4,2,120,640]{3,2,1,0:T(8,128)(2,1)}, bf16[2,120,512]{2,1,0:T(8,128)(2,1)}) custom-call(bf16[2,2,2,120,2560]{4,3,2,1,0:T(8,128)(2,1)} %bitcast.222, bf16[2,2,2,120,2560]{4,3,2,1,0:T(8,128)(2,1)} %bitcast.221, bf16[2,2,2,120,2560]{4,3,2,1,0:T(8,128)(2,1)} %bitcast.220, ...), custom_call_target="tpu_custom_call" | custom-call | tf_op jit(solution)/shard_map/pallas_call | solution.py:574
  290.4 1.1 copy.79
  291.5 0.6 convert_multiply_fusion.5
  292.2 1.2 fusion.79
  293.7 0.9 multiply_bitcast_fusion.2
  294.6 1.7 convert_multiply_fusion
  296.4 1.5 multiply_bitcast_fusion
  298.0 2.9 convert_multiply_fusion.1
  (94 shorter events, 2.6 us)
Async XLA Ops:
  9.5 1.3 copy-start.1
  10.7 1.3 copy-start.2
  12.0 53.1 %copy-start.3 = (bf16[1,160,960]{2,1,0:T(8,128)(2,1)S(1)}, bf16[1,160,960]{2,1,0:T(8,128)(2,1)}, u32[]{:S(2)}) copy-start(bf16[1,160,960]{2,1,0:T(8,128)(2,1)} %param.11) | copy-start | bytes 921604
  62.7 2.3 copy-start
  69.2 6.7 %copy-start.24 = (bf16[160,5,32]{0,2,1:T(8,128)(2,1)}, bf16[160,5,32]{0,2,1:T(8,128)(2,1)S(1)}, u32[]{:S(2)}) copy-start(bf16[160,5,32]{0,2,1:T(8,128)(2,1)S(1)} %get-tuple-element.46) | copy-start | bytes 153604
  69.2 6.7 %copy-start.26 = (bf16[160,5,32]{0,2,1:T(8,128)(2,1)}, bf16[160,5,32]{0,2,1:T(8,128)(2,1)S(1)}, u32[]{:S(2)}) copy-start(bf16[160,5,32]{0,2,1:T(8,128)(2,1)S(1)} %get-tuple-element.47) | copy-start | bytes 153604
  73.4 2.5 copy-start.28
  75.8 0.7 copy-start.20
  75.9 0.8 copy-start.22
  76.6 4.0 %slice-start.2 = ((s8[4915200]{0:T(1024)(128)(4,1)}), s8[4194304]{0:T(1024)(128)(4,1)S(1)}, s32[]{:S(2)}) async-start(s8[4915200]{0:T(1024)(128)(4,1)} %bitcast.223), calls=%async_computation.2 | async-start | bytes 8388608
  77.0 3.6 %slice-start.3 = ((s8[4915200]{0:T(1024)(128)(4,1)}), s8[720896]{0:T(1024)(128)(4,1)S(1)}, s32[]{:S(2)}) async-start(s8[4915200]{0:T(1024)(128)(4,1)} %bitcast.223), calls=%async_computation.3 | async-start | bytes 1441792
  77.1 4.7 %slice-start.4 = ((s8[4915200]{0:T(1024)(128)(4,1)}), s8[4194304]{0:T(1024)(128)(4,1)S(1)}, s32[]{:S(2)}) async-start(s8[4915200]{0:T(1024)(128)(4,1)} %bitcast.227), calls=%async_computation.4 | async-start | bytes 8388608
  77.6 2.9 copy-start.16
  80.5 9.0 %copy-start.4 = (f32[1,160,960]{2,1,0:T(8,128)}, f32[1,160,960]{2,1,0:T(8,128)S(1)}, u32[]{:S(2)}) copy-start(f32[1,160,960]{2,1,0:T(8,128)S(1)} %get-tuple-element.58) | copy-start | bytes 1843204
  80.5 1.5 slice-start.5
  80.5 2.8 slice-start.6
  80.7 2.8 slice-start.7
  82.0 1.6 copy-start.17
  85.9 1.9 copy-start.8
  85.9 1.9 copy-start.12
  85.9 3.5 %copy-start.14 = (bf16[160,2560]{1,0:T(8,128)(2,1)}, bf16[160,2560]{1,0:T(8,128)(2,1)S(1)}, u32[]{:S(2)}) copy-start(bf16[160,2560]{1,0:T(8,128)(2,1)S(1)} %get-tuple-element.37) | copy-start | bytes 2457604
  93.7 0.8 copy-start.6
  104.7 3.2 %copy-start.10 = (bf16[160,960]{0,1:T(8,128)(2,1)S(1)}, bf16[160,960]{0,1:T(8,128)(2,1)}, u32[]{:S(2)}) copy-start(bf16[160,960]{0,1:T(8,128)(2,1)} %copy.59) | copy-start | bytes 921604
  108.6 0.9 copy-start.21
  108.6 1.1 copy-start.23
  108.6 1.6 copy-start.25
  108.6 1.6 copy-start.27
  108.6 2.2 slice-start
  109.6 2.3 slice-start.1
  112.7 1.5 copy-start.7
  117.2 3.3 %copy-start.5 = (bf16[960,960]{1,0:T(8,128)(2,1)S(1)}, bf16[960,960]{1,0:T(8,128)(2,1)}, u32[]{:S(2)}) copy-start(bf16[960,960]{1,0:T(8,128)(2,1)} %convolution_convert_fusion.3) | copy-start | bytes 5529604
  120.4 8.4 %copy-start.9 = (bf16[160,2560]{1,0:T(8,128)(2,1)S(1)}, bf16[160,2560]{1,0:T(8,128)(2,1)}, u32[]{:S(2)}) copy-start(bf16[160,2560]{1,0:T(8,128)(2,1)} %copy-done.8) | copy-start | bytes 2457604
  120.4 8.4 %copy-start.18 = (bf16[1,160,960]{2,1,0:T(8,128)(2,1)S(1)}, bf16[1,160,960]{2,1,0:T(8,128)(2,1)}, u32[]{:S(2)}) copy-start(bf16[1,160,960]{2,1,0:T(8,128)(2,1)} %param.12) | copy-start | bytes 921604
  128.8 3.7 %copy-start.15 = (bf16[160,2560]{1,0:T(8,128)(2,1)S(1)}, bf16[160,2560]{1,0:T(8,128)(2,1)}, u32[]{:S(2)}) copy-start(bf16[160,2560]{1,0:T(8,128)(2,1)} %copy-done.14) | copy-start | bytes 2457604
  132.5 3.8 %copy-start.13 = (bf16[160,2560]{1,0:T(8,128)(2,1)S(1)}, bf16[160,2560]{1,0:T(8,128)(2,1)}, u32[]{:S(2)}) copy-start(bf16[160,2560]{1,0:T(8,128)(2,1)} %copy-done.12) | copy-start | bytes 2457604
  290.4 4.2 %copy-start.19 = (bf16[4,2,120,640]{3,2,1,0:T(8,128)(2,1)S(1)}, bf16[4,2,120,640]{3,2,1,0:T(8,128)(2,1)}, u32[]{:S(2)}) copy-start(bf16[4,2,120,640]{3,2,1,0:T(8,128)(2,1)} %get-tuple-element.25) | copy-start | bytes 3686404
  293.6 2.8 copy-start.11

commit v3 on v2

--- a/solution.py
+++ b/solution.py
@@ -208,7 +208,6 @@
     )
     grad_resid_mid = cotangent.astype(jnp.float32) + grad_norm_two
     grad_mid_bf = grad_resid_mid.astype(jnp.bfloat16).reshape(-1, width)
-    sum_output = matmul_tn(flat_mixed, grad_mid_bf)
     grad_mixed_bf = (
         matmul_nt(grad_mid_bf, w_output)
         .astype(jnp.bfloat16)
@@ -230,9 +229,28 @@
     value_gradient_low = value_gradient.astype(jnp.bfloat16).reshape(
         -1, KEY_VALUE_HEADS * HEAD_DIMENSION
     )
-    sum_query = matmul_tn(flattened_first, grad_query_bf)
-    sum_key = matmul_tn(flattened_first, key_gradient_low)
-    sum_value = matmul_tn(flattened_first, value_gradient_low)
+    kv_width = key_gradient_low.shape[1]
+    sum_attn = matmul_tn(
+        jnp.concatenate([flattened_first, flat_mixed], axis=0),
+        jnp.concatenate(
+            [
+                jnp.concatenate(
+                    [
+                        grad_query_bf,
+                        key_gradient_low,
+                        jnp.zeros_like(grad_mid_bf),
+                        value_gradient_low,
+                    ],
+                    axis=1,
+                ),
+                jnp.pad(
+                    grad_mid_bf,
+                    ((0, 0), (grad_query_bf.shape[1] + kv_width, kv_width)),
+                ),
+            ],
+            axis=0,
+        ),
+    )
     grad_normed_one = (
         matmul_nt(grad_query_bf, w_query)
         + matmul_nt(key_gradient_low, key_weight)
@@ -245,10 +263,7 @@
     return (
         grad_inputs,
         (
-            sum_query,
-            sum_key,
-            sum_value,
-            sum_output,
+            sum_attn,
             sum_gate,
             sum_up,
             sum_down,
@@ -511,8 +526,8 @@
             landed_inner(t, k).wait_recv()
         start_store(t)
 
-    lags = ((stage_core, 0), (stage_pair, 4), (stage_inner, 6), (stage_outer, 8),
-            (stage_spread, 10), (stage_store, 12))
+    lags = ((stage_core, 0), (stage_pair, 3), (stage_inner, 4), (stage_outer, 5),
+            (stage_spread, 6), (stage_store, 7))
 
     def step(s, carry):
         for stage, lag in lags:
@@ -521,7 +536,7 @@
                 stage(s - lag)
         return carry
 
-    lax.fori_loop(0, steps + 12, step, 0)
+    lax.fori_loop(0, steps + 7, step, 0)
 
     def drain(t, carry):
         core_copy(t, sources[0], 0).wait_send()
@@ -846,15 +861,12 @@
     grad_inputs, grads = backward_pass(cotangent, gathered, saved)
     scale = float(n_copies * n_group * inputs.shape[0] * inputs.shape[1]) ** (-0.5)
     bf = jnp.bfloat16
-    attn_block = jnp.concatenate(
-        [g.astype(bf) for g in (grads[0], grads[1], grads[3], grads[2])], axis=1
-    )
     gain_block = jnp.concatenate(
-        [g.astype(bf).reshape(n_group, rows) for g in (grads[7], grads[8])], axis=1
+        [g.astype(bf).reshape(n_group, rows) for g in (grads[4], grads[5])], axis=1
     )
     big, down_sum, gain_sum = reduce_blocks(
-        (attn_block, grads[4].astype(bf), grads[5].astype(bf)),
-        grads[6].astype(bf),
+        (grads[0].astype(bf), grads[1].astype(bf), grads[2].astype(bf)),
+        grads[3].astype(bf),
         gain_block,
         n_copies,
         n_group,

time: 302 us -> 286 us (0.947)
  local copies, waits for them, and re-layouts: 38.1 us -> 27.5 us
  Pallas kernels: 201 us -> 193 us
    pallas_call x1, Pallas kernels: 150 us -> 142 us  [reduce_blocks(): pl.pallas_call(functools.partial(reduce_kernel, n_copies, n_group, per_bl...]
    concatenate x1, local copies, waits for them, and re-layouts: 8.35 us -> 0.39 us  [backward_pass(): jnp.concatenate([grad_query_bf, key_gradient_low, jnp.zeros_like(grad_mid...]
    dot_general x7, matrix products: 11.1 us -> 15.6 us  [matrix_product(): jnp.dot(left_matrix, right_matrix, preferred_element_type=jnp.float32)]
    dot_general x7 -> x4, matrix products: 18.2 us -> 15.6 us  [matmul_tn(): lax.dot_general(left_matrix, right_matrix, (((0,), (0,)), ((), ())), pref...]
    unnamed x82 -> x124, local copies, waits for them, and re-layouts: 14.4 us -> 13.5 us
where the time goes in v3:
time: 286 us; the launch traced here: 285 us
  Pallas kernels  193 us (67%)
  matrix products  47.1 us (16%)
  local copies, waits for them, and re-layouts  27.5 us (10%)
  other arithmetic  16.1 us (6%)
    pallas_call x1, Pallas kernels, reduce_blocks(): pl.pallas_call(functools.partial(reduce_kernel, n_copies, n_group, per_bl...  142 us
    pallas_call x1, Pallas kernels, gather_weights(): pl.pallas_call(functools.partial(gather_kernel, n_copies, n_group), out_s...  50.6 us
    dot_general x4, matrix products, matmul_tn(): lax.dot_general(left_matrix, right_matrix, (((0,), (0,)), ((), ())), pref...  15.6 us
    dot_general x7, matrix products, matrix_product(): jnp.dot(left_matrix, right_matrix, preferred_element_type=jnp.float32)  15.6 us
    unnamed x124, local copies, waits for them, and re-layouts  13.5 us
    dot_general x7, matrix products, matmul_nt(): lax.dot_general(left_matrix, right_matrix, (((1,), (1,)), ((), ())), pref...  11.6 us
    mul x5, other arithmetic, scaled(): return value.astype(jnp.float32) * scale  10.6 us
    dot_general x4, local copies, waits for them, and re-layouts, matrix_product(): jnp.dot(left_matrix, right_matrix, preferred_element_type=jnp.float32)  6.11 us

profile of v3, /device:TPU:0, one launch (start us, length us, event | category | flops | bytes accessed | tf_op | source)
XLA Modules:
  0.0 285.2 jit_solution(2523081955774703285)
XLA Ops:
  0.6 1.1 copy.39
  1.7 1.1 copy.40
  2.8 2.3 concatenate.55.refs_0_
  5.1 1.6 copy.41.refs_3_
  6.8 1.3 copy-done.1
  8.1 1.3 copy-done.2
  9.4 50.6 %shard_map.194 = (bf16[4,240,2560]{2,1,0:T(8,128)(2,1)S(1)}, bf16[4,240,2560]{2,1,0:T(8,128)(2,1)}, bf16[4,240,2560]{2,1,0:T(8,128)(2,1)}, bf16[4,640,960]{2,1,0:T(8,128)(2,1)}, bf16[4,16,128]{2,1,0:T(8,128)(2,1)S(1)}) custom-call(bf16[240,2560]{1,0:T(8,128)(2,1)S(1)} %concatenate.55.refs_0_, bf16[240,2560]{1,0:T(8,128)(2,1)S(1)} %copy-done.1, ...), custom_call_target="tpu_custom_call" | custom-call | tf_op jit(solution)/shard_map/pallas_call | solution.py:798
  60.1 2.3 copy-done
  62.3 0.7 slice_convert_fusion
  63.1 0.1 fusion.45
  63.3 1.6 convolution_convert_fusion.5
  65.0 1.8 slice_bitcast_fusion
  66.8 2.4 copy.44
  69.2 2.3 convolution_bitcast_fusion.1
  71.5 0.8 broadcast_multiply_fusion
  72.5 1.7 slice_bitcast_fusion.1
  74.2 0.3 copy.43
  74.5 0.4 convolution_bitcast_fusion.3
  75.0 0.6 fusion.84
  75.7 0.4 exponential_reduce_fusion
  76.1 0.5 convolution_convert_fusion.4
  76.7 2.4 multiply_reduce_fusion
  79.3 3.6 %fusion.85 = f32[160,2560]{1,0:T(8,128)S(1)} fusion(bf16[160,960]{1,0:T(8,128)(2,1)S(1)} %fusion.56, bf16[960,2560]{1,0:T(8,128)(2,1)} %bitcast.219), kind=kOutput, calls=%fused_computation.143 | convolution fusion | flops 786432000 | bytes 6860800 | tf_op jit(solution)/shard_map/dot_general | solution.py:20
  82.9 3.6 %fusion.86 = f32[160,2560]{1,0:T(8,128)S(1)} fusion(bf16[160,960]{1,0:T(8,128)(2,1)S(1)} %fusion.56, bf16[960,2560]{1,0:T(8,128)(2,1)} %bitcast.215), kind=kOutput, calls=%fused_computation.144 | convolution fusion | flops 786432000 | bytes 6860800 | tf_op jit(solution)/shard_map/dot_general | solution.py:20
  86.5 2.4 multiply_convert_fusion
  89.0 1.8 fusion.28
  90.8 1.7 fusion.87
  92.5 2.3 fusion.49
  94.8 0.8 copy-done.3
  95.6 0.2 convert_bitcast_fusion
  95.9 0.7 copy-done.36
  96.6 3.1 %fusion.29 = bf16[160,960]{1,0:T(8,128)(2,1)} fusion(bf16[160,960]{1,0:T(8,128)(2,1)S(1)} %convert_bitcast_fusion, bf16[960,2560]{1,0:T(8,128)(2,1)} %bitcast.205), kind=kOutput, calls=%fused_computation.50 | convolution fusion | flops 295065600 | bytes 2580480 | tf_op jit(solution)/shard_map/dot_general | solution.py:30
  99.6 2.0 copy.46
  101.6 1.8 fusion.1
  103.4 0.9 fusion.27
  104.3 0.1 copy-done.32
  104.5 0.3 fusion.63
  104.8 0.1 subtract_convert_fusion
  105.1 0.6 slice-done
  105.7 0.2 slice-done.1
  105.8 0.7 fusion.12
  106.6 0.5 convolution_bitcast_fusion.5
  107.3 0.7 copy-done.24
  107.9 0.6 convolution_add_fusion.1
  108.6 0.6 fusion.32
  109.3 0.8 fusion.44
  110.1 1.4 fusion.82
  111.5 0.2 copy.51
  111.8 1.0 copy.53
  112.9 0.4 concatenate.66
  113.3 0.2 copy.50
  113.5 4.4 %convolution_convert_fusion = bf16[960,2560]{1,0:T(8,128)(2,1)} fusion(bf16[160,960]{1,0:T(8,128)(2,1)S(1)} %copy-done.37, bf16[160,2560]{1,0:T(8,128)(2,1)S(1)} %concatenate.66, bf16[160,960]{1,0:T(8,128)(2,1)S(1)} %copy.50, bf16[160,960]{1,0:T(8,128)(2,1)S(1)} %copy-done.35), kind=kOutput, calls=%fused_computation | convolution fusion | flops 1581465600 | bytes 6656000 | tf_op jit(solution)/shard_map/dot_general | solution.py:24
  117.9 3.7 %convolution_convert_fusion.3 = bf16[960,2560]{1,0:T(8,128)(2,1)} fusion(bf16[160,960]{1,0:T(8,128)(2,1)S(1)} %fusion.56, bf16[160,2560]{1,0:T(8,128)(2,1)S(1)} %copy-done.11), kind=kOutput, calls=%fused_computation.3 | convolution fusion | flops 788889600 | bytes 6041600 | tf_op jit(solution)/shard_map/dot_general | solution.py:24
  121.7 3.7 %convolution_convert_fusion.2 = bf16[960,2560]{1,0:T(8,128)(2,1)} fusion(bf16[160,960]{1,0:T(8,128)(2,1)S(1)} %fusion.56, bf16[160,2560]{1,0:T(8,128)(2,1)S(1)} %copy-done.9), kind=kOutput, calls=%fused_computation.2 | convolution fusion | flops 788889600 | bytes 6041600 | tf_op jit(solution)/shard_map/dot_general | solution.py:24
  125.4 3.7 %convolution_convert_fusion.1 = bf16[2560,960]{0,1:T(8,128)(2,1)} fusion(bf16[160,2560]{1,0:T(8,128)(2,1)S(1)} %copy-done.6, bf16[1,160,960]{2,1,0:T(8,128)(2,1)S(1)} %copy-done.14), kind=kOutput, calls=%fused_computation.1 | convolution fusion | flops 788889600 | bytes 6041600 | tf_op jit(solution)/shard_map/dot_general | solution.py:24
  129.4 0.3 fusion.33
  129.6 1.1 copy.67
  130.7 142.3 %shard_map.195 = (bf16[3,2,120,2560]{3,2,1,0:T(8,128)(2,1)}, bf16[4,2,120,640]{3,2,1,0:T(8,128)(2,1)}, bf16[2,120,512]{2,1,0:T(8,128)(2,1)}) custom-call(bf16[2,2,2,120,2560]{4,3,2,1,0:T(8,128)(2,1)} %bitcast.227, bf16[2,2,2,120,2560]{4,3,2,1,0:T(8,128)(2,1)} %bitcast.212, bf16[2,2,2,120,2560]{4,3,2,1,0:T(8,128)(2,1)} %bitcast.213, ...), custom_call_target="tpu_custom_call" | custom-call | tf_op jit(solution)/shard_map/pallas_call | solution.py:589
  273.0 2.7 multiply_bitcast_fusion
  275.7 1.2 fusion.83
  277.2 0.9 multiply_bitcast_fusion.2
  278.1 4.7 %convert_multiply_fusion.1 = (f32[1,2,120,2560]{3,2,1,0:T(8,128)}, f32[1,2,120,2560]{3,2,1,0:T(8,128)}) fusion(bf16[3,2,120,2560]{3,2,1,0:T(8,128)(2,1)} %get-tuple-element.24), kind=kLoop, calls=%fused_computation.15 | loop fusion | flops 2457600 | bytes 7372800 | tf_op jit(solution)/shard_map/mul | solution.py:876
  282.8 1.7 convert_multiply_fusion
  284.5 0.6 convert_multiply_fusion.5
  (136 shorter events, 1.9 us)
Async XLA Ops:
  2.8 4.0 %copy-start.48 = (bf16[240]{0:T(256)(128)(2,1)S(1)}, bf16[240]{0:T(256)(128)(2,1)}, u32[]{:S(2)}) copy-start(bf16[240]{0:T(256)(128)(2,1)} %param.21) | copy-start | bytes 1444
  2.8 4.0 %copy-start.49 = (bf16[240]{0:T(256)(128)(2,1)S(1)}, bf16[240]{0:T(256)(128)(2,1)}, u32[]{:S(2)}) copy-start(bf16[240]{0:T(256)(128)(2,1)} %param.20) | copy-start | bytes 1444
  6.8 1.3 copy-start.1
  8.1 1.3 copy-start.2
  9.4 53.7 %copy-start.15 = (bf16[1,160,960]{2,1,0:T(8,128)(2,1)S(1)}, bf16[1,160,960]{2,1,0:T(8,128)(2,1)}, u32[]{:S(2)}) copy-start(bf16[1,160,960]{2,1,0:T(8,128)(2,1)} %param.11) | copy-start | bytes 921604
  60.0 2.3 copy-start
  63.1 11.4 %copy-start.40 = (f32[960]{0:T(1024)}, f32[960]{0:T(1024)S(1)}, u32[]{:S(2)}) copy-start(f32[960]{0:T(1024)S(1)} %reshape.407) | copy-start | bytes 11524
  63.3 11.2 %copy-start.43 = (f32[160]{0:T(256)}, f32[160]{0:T(256)S(1)}, u32[]{:S(2)}) copy-start(f32[160]{0:T(256)S(1)} %add_rsqrt_fusion.1) | copy-start | bytes 1924
  65.0 11.1 %copy-start.22 = (bf16[160,320]{0,1:T(8,128)(2,1)}, bf16[160,320]{0,1:T(8,128)(2,1)S(1)}, u32[]{:S(2)}) copy-start(bf16[160,320]{0,1:T(8,128)(2,1)S(1)} %copy.42) | copy-start | bytes 307204
  72.5 3.2 %copy-start.27 = (bf16[1,160,15,32]{1,3,2,0:T(8,128)(2,1)}, bf16[1,160,15,32]{1,3,2,0:T(8,128)(2,1)S(1)}, u32[]{:S(2)}) copy-start(bf16[1,160,15,32]{1,3,2,0:T(8,128)(2,1)S(1)} %get-tuple-element.42) | copy-start | bytes 460804
  72.5 3.2 %copy-start.29 = (bf16[1,160,15,32]{1,3,2,0:T(8,128)(2,1)}, bf16[1,160,15,32]{1,3,2,0:T(8,128)(2,1)S(1)}, u32[]{:S(2)}) copy-start(bf16[1,160,15,32]{1,3,2,0:T(8,128)(2,1)S(1)} %get-tuple-element.43) | copy-start | bytes 460804
  75.0 0.7 copy-start.33
  75.0 1.1 copy-start.31
  75.7 1.0 copy-start.16
  76.7 2.4 copy-start.18
  76.7 2.4 copy-start.42
  79.2 7.3 %slice-start.6 = ((s8[5242880]{0:T(1024)(128)(4,1)}), s8[4194304]{0:T(1024)(128)(4,1)S(1)}, s32[]{:S(2)}) async-start(s8[5242880]{0:T(1024)(128)(4,1)} %bitcast.223), calls=%async_computation.6 | async-start | bytes 8388608
  79.3 7.2 %slice-start.7 = ((s8[5242880]{0:T(1024)(128)(4,1)}), s8[1048576]{0:T(1024)(128)(4,1)S(1)}, s32[]{:S(2)}) async-start(s8[5242880]{0:T(1024)(128)(4,1)} %bitcast.223), calls=%async_computation.7 | async-start | bytes 2097152
  79.3 7.2 %copy-start.12 = (bf16[1,160,960]{2,1,0:T(8,128)(2,1)S(1)}, bf16[1,160,960]{2,1,0:T(8,128)(2,1)}, u32[]{:S(2)}) copy-start(bf16[1,160,960]{2,1,0:T(8,128)(2,1)} %param.12) | copy-start | bytes 921604
  82.9 7.9 %slice-start.4 = ((s8[4915200]{0:T(1024)(128)(4,1)}), s8[4194304]{0:T(1024)(128)(4,1)S(1)}, s32[]{:S(2)}) async-start(s8[4915200]{0:T(1024)(128)(4,1)} %bitcast.220), calls=%async_computation.4 | async-start | bytes 8388608
  82.9 9.5 %slice-start.2 = ((s8[4915200]{0:T(1024)(128)(4,1)}), s8[4194304]{0:T(1024)(128)(4,1)S(1)}, s32[]{:S(2)}) async-start(s8[4915200]{0:T(1024)(128)(4,1)} %bitcast.216), calls=%async_computation.2 | async-start | bytes 8388608
  86.5 4.2 %slice-start.5 = ((s8[4915200]{0:T(1024)(128)(4,1)}), s8[720896]{0:T(1024)(128)(4,1)S(1)}, s32[]{:S(2)}) async-start(s8[4915200]{0:T(1024)(128)(4,1)} %bitcast.220), calls=%async_computation.5 | async-start | bytes 1441792
  86.5 5.9 %slice-start.3 = ((s8[4915200]{0:T(1024)(128)(4,1)}), s8[720896]{0:T(1024)(128)(4,1)S(1)}, s32[]{:S(2)}) async-start(s8[4915200]{0:T(1024)(128)(4,1)} %bitcast.216), calls=%async_computation.3 | async-start | bytes 1441792
  89.0 1.8 copy-start.5
  89.0 1.8 copy-start.10
  89.0 3.5 %copy-start.8 = (bf16[160,2560]{1,0:T(8,128)(2,1)}, bf16[160,2560]{1,0:T(8,128)(2,1)S(1)}, u32[]{:S(2)}) copy-start(bf16[160,2560]{1,0:T(8,128)(2,1)S(1)} %get-tuple-element.37) | copy-start | bytes 2457604
  94.8 0.8 copy-start.3
  94.8 4.9 %copy-start.45 = (f32[160]{0:T(256)}, f32[160]{0:T(256)S(1)}, u32[]{:S(2)}) copy-start(f32[160]{0:T(256)S(1)} %broadcast_multiply_fusion.2) | copy-start | bytes 1924
  95.9 0.7 copy-start.36
  103.4 2.3 slice-start
  103.4 1.0 copy-start.32
  103.4 1.1 copy-start.34
  103.4 1.4 copy-start.38
  103.4 2.4 slice-start.1
  104.9 1.7 copy-start.28
  105.0 1.7 copy-start.30
  105.1 2.1 copy-start.20
  106.6 2.0 copy-start.7
  107.3 0.7 copy-start.24
  107.9 1.3 copy-start.17
  107.9 1.3 copy-start.41
  107.9 1.3 copy-start.44
  108.6 1.5 copy-start.4
  108.6 1.5 copy-start.13
  108.6 1.4 copy-start.46
  109.2 2.3 copy-start.23
  109.2 2.2 copy-start.21
  110.0 1.6 copy-start.25
  111.5 1.8 copy-start.19
  111.5 2.0 copy-start.35
  111.5 2.0 copy-start.37
  113.5 4.4 %copy-start.11 = (bf16[160,2560]{1,0:T(8,128)(2,1)S(1)}, bf16[160,2560]{1,0:T(8,128)(2,1)}, u32[]{:S(2)}) copy-start(bf16[160,2560]{1,0:T(8,128)(2,1)} %copy-done.10) | copy-start | bytes 2457604
  117.9 3.8 %copy-start.9 = (bf16[160,2560]{1,0:T(8,128)(2,1)S(1)}, bf16[160,2560]{1,0:T(8,128)(2,1)}, u32[]{:S(2)}) copy-start(bf16[160,2560]{1,0:T(8,128)(2,1)} %copy-done.8) | copy-start | bytes 2457604
  121.7 3.7 %copy-start.6 = (bf16[160,2560]{1,0:T(8,128)(2,1)S(1)}, bf16[160,2560]{1,0:T(8,128)(2,1)}, u32[]{:S(2)}) copy-start(bf16[160,2560]{1,0:T(8,128)(2,1)} %copy-done.5) | copy-start | bytes 2457604
  121.7 3.7 %copy-start.14 = (bf16[1,160,960]{2,1,0:T(8,128)(2,1)S(1)}, bf16[1,160,960]{2,1,0:T(8,128)(2,1)}, u32[]{:S(2)}) copy-start(bf16[1,160,960]{2,1,0:T(8,128)(2,1)} %param.12) | copy-start | bytes 921604
  125.4 3.7 %copy-start.47 = (bf16[960]{0:T(1024)(128)(2,1)S(1)}, bf16[960]{0:T(1024)(128)(2,1)}, u32[]{:S(2)}) copy-start(bf16[960]{0:T(1024)(128)(2,1)} %get-tuple-element.27) | copy-start | bytes 5764
  278.1 4.7 %copy-start.26 = (bf16[4,2,120,640]{3,2,1,0:T(8,128)(2,1)S(1)}, bf16[4,2,120,640]{3,2,1,0:T(8,128)(2,1)}, u32[]{:S(2)}) copy-start(bf16[4,2,120,640]{3,2,1,0:T(8,128)(2,1)} %get-tuple-element.25) | copy-start | bytes 3686404
  282.8 1.7 copy-start.39
